TPU v7x, 32 devices: a whole 2x2x4 slice. The times are simulated.
32 devices in a mesh: grp: 2 (over y), keys: 4 (over x, core), qry: 4 (over z).
Axes of the slice: x: 2, y: 2, z: 4, core: 2. Of those that a mesh axis runs over, the one named last changes fastest.
Arguments:
- queries: bfloat16 [4096, 8, 128], P(('grp', 'keys', 'qry')), parts along dimension 0, may hold values from -40 to 40, as said below
- cache_keys: bfloat16 [4096, 128], P(('grp', 'keys')), parts along dimension 0, may hold values from -128 to 128, as said below
- cache_values: bfloat16 [4096, 128], P(('grp', 'keys')), parts along dimension 0, may hold values from -24 to 24
- entry: int32 [8, 4], P(('grp', 'keys'), 'qry'), parts along dimension 0, may hold values from 0 to 3
- visits: int32 [8, 4], P(('grp', 'keys'), 'qry'), parts along dimension 0, may hold values from 3 to 4
- doc_length: int32 [2], P('grp'), parts along dimension 0, may hold values from 1025 to 2048
- slot_params: float32 [2048, 256], P(('grp', 'keys', 'qry')), parts along dimension 0, may hold values from -128 to 128, as said below
- first_moment: float32 [2048, 256], P(('grp', 'keys', 'qry')), parts along dimension 0, may hold values from -3 to 3
- second_moment: float32 [2048, 256], P(('grp', 'keys', 'qry')), parts along dimension 0, may hold values from 0.05 to 1
Outputs:
- teacher_out: bfloat16 [4096, 8, 128], P(('grp', 'keys', 'qry')), parts along dimension 0
- slot_grad: float32 [2048, 256], P(('grp', 'keys', 'qry')), parts along dimension 0
- new_params: float32 [2048, 256], P(('grp', 'keys', 'qry')), parts along dimension 0
- new_first: float32 [2048, 256], P(('grp', 'keys', 'qry')), parts along dimension 0
- new_second: float32 [2048, 256], P(('grp', 'keys', 'qry')), parts along dimension 0
- loss: float32 [2], P('grp'), parts along dimension 0
There are 2 independent parts, one for each index of `grp`. A program takes and returns all parts, laid end to end along the dimension named above; each array names one. Nothing has to cross between parts.
Inputs may be any that keep to these rules, and one draw needn't show every extreme that they name: `queries`: query entries stay within the stated range. `cache_keys`: cache key entries stay within the stated range. `slot_params`: slot entries stay within the stated range.
All inputs are finite; a program needn't handle non-finite values.
Results may differ from a plain program's by a relative error of at most 0.0045.
Values may be sent and summed in bfloat16 or wider, within the bound.
No kernel may reach another device: no remote copies, remote signals or barrier semaphores. Data moves between devices by JAX's collectives and lax.ppermute only.
A program may use at most 64 MiB of HBM per device.

v0:
```python
import math

import jax
import jax.numpy as jnp
from jax import lax
from jax.experimental import pallas as pl
from jax.experimental.pallas import tpu as pltpu
from jax.sharding import PartitionSpec as P


NEG = -1e30
PAD = 8
LANES = 128
GRANT = 24 * 2**20


def nt(left, right):
    return lax.dot_general(left, right, (((1,), (1,)), ((), ())), preferred_element_type=jnp.float32)


def nn(left, right):
    return jnp.dot(left, right, preferred_element_type=jnp.float32)


def with_ones(values):
    turned = values.T
    return jnp.concatenate([turned, jnp.ones((PAD, turned.shape[1]), turned.dtype)], axis=0)


def row_block(rows):
    return math.gcd(rows, 256)


def call(kernel, out, scalars, arrays, scratch=(), hbm_out=()):
    vm = pl.BlockSpec(memory_space=pltpu.VMEM)
    sm = pl.BlockSpec(memory_space=pltpu.SMEM)
    arrays = [pltpu.with_memory_space_constraint(a, pltpu.VMEM) for a in arrays]
    shapes = tuple(
        jax.ShapeDtypeStruct(s, d) if i in hbm_out else pltpu.VMEM(s, d) for i, (s, d) in enumerate(out)
    )
    return pl.pallas_call(
        kernel,
        out_shape=shapes,
        in_specs=[sm] * len(scalars) + [vm] * len(arrays),
        out_specs=tuple(vm for _ in shapes),
        scratch_shapes=list(scratch),
        compiler_params=pltpu.CompilerParams(vmem_limit_bytes=GRANT),
    )(*scalars, *arrays)


def load(queries, keys, values, slot_params):
    size, width = keys.shape
    ins = [pltpu.with_memory_space_constraint(a, pltpu.HBM) for a in (slot_params, keys, values, queries)]

    def kernel(*refs):
        sources, (slots_ref, cache_ref, q_ref, full_ref, sems) = refs[:4], refs[4:]
        targets = (full_ref, cache_ref.at[pl.ds(0, size)], cache_ref.at[pl.ds(size, size)], q_ref)
        moves = [pltpu.make_async_copy(a, b, sems.at[i]) for i, (a, b) in enumerate(zip(sources, targets))]
        for move in moves:
            move.start()
        moves[0].wait()
        slots_ref[...] = full_ref[...].astype(jnp.bfloat16)
        for move in moves[1:]:
            move.wait()

    return pl.pallas_call(
        kernel,
        out_shape=(
            pltpu.VMEM(slot_params.shape, jnp.bfloat16),
            pltpu.VMEM((2 * size, width), keys.dtype),
            pltpu.VMEM(queries.shape, queries.dtype),
        ),
        in_specs=[pl.BlockSpec(memory_space=pltpu.HBM)] * 4,
        out_specs=(pl.BlockSpec(memory_space=pltpu.VMEM),) * 3,
        scratch_shapes=[
            pltpu.VMEM(slot_params.shape, slot_params.dtype),
            pltpu.SemaphoreType.DMA((4,)),
        ],
        compiler_params=pltpu.CompilerParams(vmem_limit_bytes=GRANT),
        name="load",
    )(*ins)


def teacher(live, queries, segments, state, last, scale):
    rows, width = queries.shape
    step = row_block(rows)
    shapes = [((1, rows), jnp.float32), ((width + PAD, rows), jnp.float32)]
    ends = [((rows, width), jnp.bfloat16), ((width, rows), jnp.bfloat16)]
    offsets = [j for j, _ in segments]
    first = state is None
    factor = scale * math.log2(math.e)

    def kernel(live_ref, q_ref, *refs):
        seg, refs = refs[: len(offsets)], refs[len(offsets):]
        if not first:
            (big_in, acc_in), refs = refs[:2], refs[2:]
        if last:
            (out_ref, outt_ref), refs = refs[:2], refs[2:]
        big_ref, acc_ref, score_ref, peak_ref = refs
        if first:
            big_ref[...] = jnp.full(big_ref.shape, NEG, jnp.float32)
            acc_ref[...] = jnp.zeros(acc_ref.shape, jnp.float32)
        else:
            big_ref[...] = big_in[...]
            acc_ref[...] = acc_in[...]
        blocks = [pl.ds(at, step) for at in range(0, rows, step)]
        for s, offset in enumerate(offsets):
            cache_ref = seg[s]
            size = cache_ref.shape[0] // 2
            count = jnp.max(live_ref[offset:offset + 1, :])

            @pl.when(count > 0)
            def _():
                live = lax.broadcasted_iota(jnp.int32, (size, width), 0) < count
                keys = jnp.where(live, cache_ref[:size, :], cache_ref[:1, :])
                turned = with_ones(cache_ref[size:, :])
                turned = jnp.where(
                    lax.broadcasted_iota(jnp.int32, turned.shape, 1) < count, turned, jnp.zeros_like(turned)
                )
                for at in blocks:
                    score = nt(keys, q_ref[at, :])
                    score_ref[:, at] = score
                    peak_ref[:, at] = jnp.max(score, axis=0, keepdims=True)
                for at in blocks:
                    big = big_ref[:, at]
                    new_big = jnp.maximum(big, peak_ref[:, at])
                    weight = jnp.exp2((score_ref[:, at] - new_big) * factor).astype(jnp.bfloat16)
                    fade = jnp.exp2((big - new_big) * factor)
                    acc_ref[:, at] = acc_ref[:, at] * fade + nn(turned, weight)
                    big_ref[:, at] = new_big

        if last:
            for i in range(rows // step):
                at = i * step
                total = acc_ref[width:width + 1, pl.ds(at, step)]
                done = (acc_ref[:width, pl.ds(at, step)] * (1.0 / total)).astype(jnp.bfloat16)
                outt_ref[:, pl.ds(at, step)] = done
                out_ref[pl.ds(at, step), :] = done.T

    arrays = [queries] + [a for _, a in segments] + ([] if first else list(state))
    scratch = [pltpu.VMEM(s, d) for s, d in shapes] if last else []
    scratch += [
        pltpu.VMEM((segments[0][1].shape[0] // 2, rows), jnp.float32), pltpu.VMEM((1, rows), jnp.float32)
    ]
    return call(
        kernel, ends if last else shapes, [], [live] + arrays, scratch,
        hbm_out=(0,) if last else (),
    )


def gradient_half(start, half, q_ref, prob_ref, cast_ref, diff_ref, inner_ref, values_ref, grad_ref, dscore_ref, scale):
    rows, width = q_ref.shape
    step = row_block(rows)
    values = values_ref[pl.ds(start, half), :]
    for at in range(0, rows, step):
        at = pl.ds(at, step)
        slope = nt(values, diff_ref[at, :]) - inner_ref[:, at]
        dscore_ref[:, at] = (prob_ref[pl.ds(start, half), at] * slope).astype(jnp.bfloat16)
    grad_ref[:, width:] = nn(cast_ref[pl.ds(start, half), :], diff_ref[...])
    grad_ref[:, :width] = nn(dscore_ref[...], q_ref[...]) * scale


def student(queries, teach, slots, other, per, half, scale):
    rounds = len(slots)
    rows, width = queries.shape
    step = row_block(rows)
    pieces = slots[0].shape[0] // per
    count = 2 * rounds * pieces * per
    factor = scale * math.log2(math.e)

    def kernel(q_ref, teach_ref, *refs):
        sources, refs = refs[: 2 * rounds], refs[2 * rounds:]
        grad_ref, prob_ref, cast_ref, diff_ref, inner_ref, values_ref, loss_ref, keys_ref, dscore_ref = refs
        n_chip, n_qry = lax.axis_size("keys") // 2, lax.axis_size("qry")
        me, mine = lax.axis_index("keys"), lax.axis_index("qry")
        core, chip = lax.rem(me, 2), lax.div(me, 2)
        for r, source in enumerate(sources):
            c, x = (core, r) if r < rounds else (1 - core, r - rounds)
            for d in range(pieces):
                place = (c * n_chip + (chip ^ x)) * n_qry + lax.rem(mine - d + n_qry, n_qry)
                to = pl.multiple_of(place * per, per)
                piece = source[pl.ds(d * per, per), :]
                keys_ref[pl.ds(to, per), :] = piece[:, :width]
                values_ref[pl.ds(to, per), :] = piece[:, width:]
        turned = with_ones(values_ref[...])
        squares = jnp.zeros((width, step), jnp.float32)
        blocks = [pl.ds(at, step) for at in range(0, rows, step)]
        for at in blocks:
            score = nt(keys_ref[...], q_ref[at, :])
            prob_ref[:, at] = score
            inner_ref[:, at] = jnp.max(score, axis=0, keepdims=True)
        for at in blocks:
            weight = jnp.exp2((prob_ref[:, at] - inner_ref[:, at]) * factor)
            prob_ref[:, at] = weight
            inner_ref[:, at] = 1.0 / jnp.sum(weight, axis=0, keepdims=True)
        for at in blocks:
            prob = prob_ref[:, at] * inner_ref[:, at]
            prob_ref[:, at] = prob
            cast = prob.astype(jnp.bfloat16)
            cast_ref[:, at] = cast
            both = nn(turned, cast)
            out, mass = both[:width, :], both[width:width + 1, :]
            diff = out - teach_ref[:, at].astype(jnp.float32)
            squares = squares + diff * diff
            short = diff.astype(jnp.bfloat16)
            diff_ref[at, :] = short.T
            inner_ref[:, at] = jnp.sum(short.astype(jnp.float32) * out, axis=0, keepdims=True) / mass
        loss_ref[...] = jnp.full(loss_ref.shape, jnp.sum(squares), jnp.float32)
        gradient_half(
            pl.multiple_of((1 - core) * half, half),
            half, q_ref, prob_ref, cast_ref, diff_ref, inner_ref, values_ref, grad_ref, dscore_ref, scale,
        )

    return call(
        kernel,
        [
            ((half, 2 * width), jnp.float32),
            ((count, rows), jnp.float32),
            ((count, rows), jnp.bfloat16),
            ((rows, width), jnp.bfloat16),
            ((1, rows), jnp.float32),
            ((count, width), jnp.bfloat16),
            ((PAD, LANES), jnp.float32),
        ],
        [], [queries, teach, *slots, *other],
        [pltpu.VMEM((count, width), jnp.bfloat16), pltpu.VMEM((half, rows), jnp.bfloat16)],
    )


def own_half(queries, prob, cast, diff, inner, values, half, scale):
    def kernel(*refs):
        start = pl.multiple_of(lax.rem(lax.axis_index("keys"), 2) * half, half)
        gradient_half(start, half, *refs, scale)

    return call(
        kernel, [((half, 2 * queries.shape[1]), jnp.float32)],
        [], [queries, prob, cast, diff, inner, values],
        [pltpu.VMEM((half, queries.shape[0]), jnp.bfloat16)],
    )[0]


def packed(own, got, loss, heard, per):
    half, wide = own.shape
    blocks = half // per

    def kernel(own_ref, got_ref, loss_ref, heard_ref, out_ref):
        squares = loss_ref[...] + heard_ref[...]
        one = squares.astype(jnp.bfloat16)
        left = squares - one.astype(jnp.float32)
        two = left.astype(jnp.bfloat16)
        three = (left - two.astype(jnp.float32)).astype(jnp.bfloat16)
        place = lax.broadcasted_iota(jnp.int32, (PAD, LANES), 0)
        zero = jnp.zeros((PAD, LANES), jnp.float32)
        parts = jnp.where(
            place == 0, one.astype(jnp.float32),
            jnp.where(place == 1, two.astype(jnp.float32), jnp.where(place == 2, three.astype(jnp.float32), zero)),
        ).astype(jnp.bfloat16)
        for b in range(blocks):
            at = b * per
            out_ref[b, :per, :] = (own_ref[pl.ds(at, per), :] + got_ref[pl.ds(at, per), :]).astype(jnp.bfloat16)
            for at in range(0, wide, LANES):
                out_ref[b, per:, pl.ds(at, LANES)] = parts

    return call(kernel, [((blocks, per + PAD, wide), jnp.bfloat16)], [], [own, got, loss, heard])[0]


def update(heard, slot_params, first_moment, second_moment, terms):
    per, wide = slot_params.shape

    def kernel(heard_ref, params_ref, first_ref, second_ref, grad_ref, p_ref, f_ref, s_ref, loss_ref):
        grad = jnp.zeros((per, wide), jnp.float32)
        tail = jnp.zeros((PAD, LANES), jnp.float32)
        for b in range(heard_ref.shape[0]):
            grad = grad + heard_ref[b, :per, :].astype(jnp.float32)
            tail = tail + heard_ref[b, per:, :LANES].astype(jnp.float32)
        grad_ref[...] = grad
        new_first = 0.9 * first_ref[...] + 0.1 * grad
        new_second = 0.95 * second_ref[...] + 0.05 * grad * grad
        f_ref[...] = new_first
        s_ref[...] = new_second
        p_ref[...] = params_ref[...] - 0.02 * new_first / (jnp.sqrt(new_second) + 1e-08)
        loss_ref[...] = jnp.sum(tail, axis=0, keepdims=True) / terms

    shape = ((per, wide), jnp.float32)
    return call(
        kernel, [shape] * 4 + [((1, LANES), jnp.float32)], [],
        [heard, slot_params, first_moment, second_moment], hbm_out=(0, 1, 2, 3, 4),
    )


def body(
    queries,
    cache_keys,
    cache_values,
    entry,
    visits,
    doc_length,
    slot_params,
    first_moment,
    second_moment,
):
    n_keys, n_qry = lax.axis_size("keys"), lax.axis_size("qry")
    tok, heads, width = queries.shape
    rows = tok * heads
    per = slot_params.shape[0]
    n_chip = n_keys // 2
    half = n_chip * n_qry * per
    scale = 1.0 / math.sqrt(width)

    def swap(block, bit):
        return lax.ppermute(block, "keys", [(k, k ^ bit) for k in range(n_keys)])

    copies, cache_own, flat = load(queries.reshape(rows, width), cache_keys, cache_values, slot_params)

    me, size = lax.axis_index("keys"), cache_keys.shape[0]
    shard = me ^ lax.broadcasted_iota(jnp.int32, (-(-n_keys // PAD) * PAD, LANES), 0)
    turn = lax.rem(shard - me - entry[0, 0] + 2 * n_keys, n_keys)
    live = jnp.where(turn < visits[0, 0], jnp.clip(doc_length[0] - shard * size, 0, size), 0)

    low = [0] + [j & -j for j in range(1, n_keys)]
    chips = range(2, n_keys, 2)

    cache = {0: cache_own}
    for j in list(chips) + list(range(1, n_keys, 2)):
        cache[j] = swap(cache[j ^ low[j]], low[j])

    column = [copies]
    for d in range(1, n_qry):
        column.append(lax.ppermute(copies, "qry", [(i, (i + d) % n_qry) for i in range(n_qry)]))
    slots = {0: jnp.concatenate(column, axis=0)}
    for j in chips:
        slots[j] = swap(slots[j ^ low[j]], low[j])
    other = [swap(slots[j], 1) for j in range(0, n_keys, 2)]
    slots = [slots[j] for j in range(0, n_keys, 2)]

    stages = [("own", [0]), ("partner", [1]), ("chip", list(chips)), ("far", list(range(3, n_keys, 2)))]
    stages = [stage for stage in stages if stage[1]]
    state = None
    for name, offsets in stages:
        last = name == stages[-1][0]
        state = teacher(live, flat, [(j, cache[j]) for j in offsets], state, last, scale)
    teacher_rows, teacher_turned = state

    away, prob, cast, diff, inner, values, loss = student(flat, teacher_turned, slots, other, per, half, scale)
    own = own_half(flat, prob, cast, diff, inner, values, half, scale)
    sent = packed(own, swap(away, 1), loss, swap(loss, 1), per)

    groups = [[(2 * x + c) * n_qry + q for x in range(n_chip) for q in range(n_qry)] for c in range(2)]
    heard = lax.all_to_all(sent, ("keys", "qry"), 0, 0, axis_index_groups=groups, tiled=True)
    slot_grad, new_params, new_first, new_second, loss = update(
        heard, slot_params, first_moment, second_moment, rows * n_keys * n_qry
    )
    teacher_out = teacher_rows.reshape(tok, heads, width)
    return (teacher_out, slot_grad, new_params, new_first, new_second, loss[0, :1])


def solution(mesh):
    return jax.shard_map(
        body,
        mesh=mesh,
        in_specs=(
            P(("grp", "keys", "qry"), None, None),
            P(("grp", "keys"), None),
            P(("grp", "keys"), None),
            P(("grp", "keys"), "qry"),
            P(("grp", "keys"), "qry"),
            P("grp"),
            P(("grp", "keys", "qry"), None),
            P(("grp", "keys", "qry"), None),
            P(("grp", "keys", "qry"), None),
        ),
        out_specs=(
            P(("grp", "keys", "qry"), None, None),
            P(("grp", "keys", "qry"), None),
            P(("grp", "keys", "qry"), None),
            P(("grp", "keys", "qry"), None),
            P(("grp", "keys", "qry"), None),
            P("grp"),
        ),
        check_vma=False,
    )
```

profile of v0, /device:TPU:0, one launch (start us, length us, event | category | flops | bytes accessed | tf_op | source)
XLA Modules:
  0.0 46.2 jit_solution(17599939667942782357)
XLA Ops:
  0.6 1.2 %load.1 = (bf16[64,256]{1,0:T(8,128)(2,1)S(1)}, bf16[1024,128]{1,0:T(8,128)(2,1)S(1)}, bf16[1024,128]{1,0:T(8,128)(2,1)S(1)}) custom-call(f32[64,256]{1,0:T(8,128)} %params_ref.1, bf16[512,128]{1,0:T(8,128)(2,1)} %refs_1_.1, bf16[512,128]{1,0:T(8,128)(2,1)} %refs_2_.1, bf16[1024,128]{1,0:T(8,128)(2,1)} %bitcast.10), custom_call_target="tpu_custom_call" | custom-call | tf_op jit(solution)/shard_map/load/pallas_call | solution.py:66
  1.8 5.1 %collective-permute-start.5 = (bf16[64,256]{1,0:T(8,128)(2,1)S(1)}, bf16[64,256]{1,0:T(8,128)(2,1)S(1)}, u32[]{:S(2)}, u32[]{:S(2)}) collective-permute-start(bf16[64,256]{1,0:T(8,128)(2,1)S(1)} %get-tuple-element.39), channel_id=1, source_target_pairs={{0,3},{1,0},{2,1},{3,2},{4,7},{5,4},{6,5},{7,6},{8,11},{9,8},{10,9... | collective-permute-start | bytes 98312 | tf_op jit(solution)/shard_map/ppermute | solution.py:329
  6.9 0.0 collective-permute-start.4
  6.9 1.0 %collective-permute-start.3 = (bf16[64,256]{1,0:T(8,128)(2,1)S(1)}, bf16[64,256]{1,0:T(8,128)(2,1)S(1)}, u32[]{:S(2)}, u32[]{:S(2)}) collective-permute-start(bf16[64,256]{1,0:T(8,128)(2,1)S(1)} %get-tuple-element.39), channel_id=1, source_target_pairs={{0,1},{1,2},{2,3},{3,0},{4,5},{5,6},{6,7},{7,4},{8,9},{9,10},{10,1... | collective-permute-start | bytes 98312 | tf_op jit(solution)/shard_map/ppermute | solution.py:329
  7.9 0.0 collective-permute-start.2
  7.9 1.5 %collective-permute-start = (bf16[1024,128]{1,0:T(8,128)(2,1)S(1)}, bf16[1024,128]{1,0:T(8,128)(2,1)S(1)}, u32[]{:S(2)}, u32[]{:S(2)}) collective-permute-start(bf16[1024,128]{1,0:T(8,128)(2,1)S(1)} %get-tuple-element.30.refs_0_), channel_id=1, source_target_pairs={{0,8},{4,12},{8,0},{12,4},{1,9},{5,13},{9,1},{13,5},{2,10},{6,14},... | collective-permute-start | bytes 786440 | tf_op jit(solution)/shard_map/ppermute | solution.py:311
  10.1 2.6 %collective-permute-done.3 = bf16[64,256]{1,0:T(8,128)(2,1)S(1)} collective-permute-done((bf16[64,256]{1,0:T(8,128)(2,1)S(1)}, bf16[64,256]{1,0:T(8,128)(2,1)S(1)}, u32[]{:S(2)}, u32[]{:S(2)}) %collective-permute-start.3) | collective-permute-done | bytes 32800 | tf_op jit(solution)/shard_map/ppermute | solution.py:329
  12.6 0.0 collective-permute-done.4
  12.7 0.0 collective-permute-done.5
  12.7 1.6 %collective-permute-start.6 = (bf16[256,256]{1,0:T(8,128)(2,1)S(1)}, bf16[256,256]{1,0:T(8,128)(2,1)S(1)}, u32[]{:S(2)}, u32[]{:S(2)}) collective-permute-start(bf16[256,256]{1,0:T(8,128)(2,1)S(1)} %constant_dynamic-update-slice_fusion.refs_0_), channel_id=1, source_target_pairs={{0,8},{4,12},{8,0},{12,4},{1,9},{5,13},{9,1},{13,5},{2,10},{6,14},... | collective-permute-start | bytes 393224 | tf_op jit(solution)/shard_map/ppermute | solution.py:311
  14.9 2.2 %collective-permute-done.refs_0_ = bf16[1024,128]{1,0:T(8,128)(2,1)S(1)} collective-permute-done((bf16[1024,128]{1,0:T(8,128)(2,1)S(1)}, bf16[1024,128]{1,0:T(8,128)(2,1)S(1)}, u32[]{:S(2)}, u32[]{:S(2)}) %collective-permute-start) | collective-permute-done | bytes 262176 | tf_op jit(solution)/shard_map/ppermute | solution.py:311
  17.1 0.0 collective-permute-start.1
  17.8 0.6 %collective-permute-start.7 = (bf16[256,256]{1,0:T(8,128)(2,1)S(1)}, bf16[256,256]{1,0:T(8,128)(2,1)S(1)}, u32[]{:S(2)}, u32[]{:S(2)}) collective-permute-start(bf16[256,256]{1,0:T(8,128)(2,1)S(1)} %constant_dynamic-update-slice_fusion.refs_0_), channel_id=1, source_target_pairs={{0,4},{4,0},{8,12},{12,8},{1,5},{5,1},{9,13},{13,9},{2,6},{6,2},{1... | collective-permute-start | bytes 393224 | tf_op jit(solution)/shard_map/ppermute | solution.py:311
  18.4 1.1 %collective-permute-done.6.refs_1_ = bf16[256,256]{1,0:T(8,128)(2,1)S(1)} collective-permute-done((bf16[256,256]{1,0:T(8,128)(2,1)S(1)}, bf16[256,256]{1,0:T(8,128)(2,1)S(1)}, u32[]{:S(2)}, u32[]{:S(2)}) %collective-permute-start.6) | collective-permute-done | bytes 131104 | tf_op jit(solution)/shard_map/ppermute | solution.py:311
  19.5 0.0 collective-permute-start.8
  19.5 0.1 fusion.1.live_ref
  19.5 1.2 %shard_map.136 = (f32[1,1024]{1,0:T(1,128)S(1)}, f32[136,1024]{1,0:T(8,128)S(1)}) custom-call(s32[8,128]{1,0:T(8,128)S(1)} %fusion.1.live_ref, bf16[1024,128]{1,0:T(8,128)(2,1)S(1)} %get-tuple-element.29.q_ref.refs_0_, bf16[1024,128]{1,0:T(8,128)(2,1)S(1)} %get-tuple-element.30.refs_0_), custom_call_target="tpu_custom_call" | custom-call | tf_op jit(solution)/shard_map/pallas_call | solution.py:41
  20.8 0.0 collective-permute-done.2.refs_0_
  20.8 1.2 %shard_map.137 = (f32[1,1024]{1,0:T(1,128)S(1)}, f32[136,1024]{1,0:T(8,128)S(1)}) custom-call(s32[8,128]{1,0:T(8,128)S(1)} %fusion.1.live_ref, bf16[1024,128]{1,0:T(8,128)(2,1)S(1)} %get-tuple-element.29.q_ref.refs_0_, bf16[1024,128]{1,0:T(8,128)(2,1)S(1)} %collective-permute-done.2.refs_0_, f32[1,1024]{1,0:T(1,128)S(1)} %get-tuple-element.31.refs_1_, ...), custom_call_target="tpu_custom_call" | custom-call | tf_op jit(solution)/shard_map/pallas_call | solution.py:41
  22.0 1.2 %shard_map.138 = (f32[1,1024]{1,0:T(1,128)S(1)}, f32[136,1024]{1,0:T(8,128)S(1)}) custom-call(s32[8,128]{1,0:T(8,128)S(1)} %fusion.1.live_ref, bf16[1024,128]{1,0:T(8,128)(2,1)S(1)} %get-tuple-element.29.q_ref.refs_0_, bf16[1024,128]{1,0:T(8,128)(2,1)S(1)} %collective-permute-done.refs_0_, f32[1,1024]{1,0:T(1,128)S(1)} %get-tuple-element.33.refs_1_, ...), custom_call_target="tpu_custom_call" | custom-call | tf_op jit(solution)/shard_map/pallas_call | solution.py:41
  23.2 0.0 collective-permute-done.1.refs_0_
  23.2 1.0 %shard_map.139 = (bf16[1024,128]{1,0:T(8,128)(2,1)}, bf16[128,1024]{1,0:T(8,128)(2,1)S(1)}) custom-call(s32[8,128]{1,0:T(8,128)S(1)} %fusion.1.live_ref, bf16[1024,128]{1,0:T(8,128)(2,1)S(1)} %get-tuple-element.29.q_ref.refs_0_, bf16[1024,128]{1,0:T(8,128)(2,1)S(1)} %collective-permute-done.1.refs_0_, f32[1,1024]{1,0:T(1,128)S(1)} %get-tuple-element.35.refs_1_, ...), custom_call_target="tpu_custom_call" | custom-call | tf_op jit(solution)/shard_map/pallas_call | solution.py:41
  24.2 0.0 collective-permute-done.7.refs_2_
  24.2 0.0 collective-permute-done.8.refs_3_
  24.2 3.2 %shard_map.140 = (f32[512,256]{1,0:T(8,128)S(1)}, f32[1024,1024]{1,0:T(8,128)S(1)}, bf16[1024,1024]{1,0:T(8,128)(2,1)S(1)}, bf16[1024,128]{1,0:T(8,128)(2,1)S(1)...) custom-call(bf16[1024,128]{1,0:T(8,128)(2,1)S(1)} %get-tuple-element.29.q_ref.refs_0_, ...), custom_call_target="tpu_custom_call" | custom-call | tf_op jit(solution)/shard_map/pallas_call | solution.py:41
  27.4 0.5 %collective-permute-start.9 = (f32[512,256]{1,0:T(8,128)S(1)}, f32[512,256]{1,0:T(8,128)S(1)}, u32[]{:S(2)}, u32[]{:S(2)}) collective-permute-start(f32[512,256]{1,0:T(8,128)S(1)} %get-tuple-element.45), channel_id=1, source_target_pairs={{0,4},{4,0},{8,12},{12,8},{1,5},{5,1},{9,13},{13,9},{2,6},{6,2},{1... | collective-permute-start | bytes 1572872 | tf_op jit(solution)/shard_map/ppermute | solution.py:311
  28.0 0.1 collective-permute-start.10
  28.1 0.0 copy-start
  28.1 0.0 copy-start.1
  28.1 0.0 copy-start.2
  28.1 1.0 %shard_map.141.own_ref = f32[512,256]{1,0:T(8,128)S(1)} custom-call(bf16[1024,128]{1,0:T(8,128)(2,1)S(1)} %get-tuple-element.29.q_ref.refs_0_, f32[1024,1024]{1,0:T(8,128)S(1)} %get-tuple-element.40.refs_1_, bf16[1024,1024]{1,0:T(8,128)(2,1)S(1)} %get-tuple-element.41.refs_2_, bf16[1024,128]{1,0:T(8,128)(2,1)S(1)} %get-tuple-element.42.refs_3_, ...), custom_call_target="tpu_custom_call" | custom-call | tf_op jit(solution)/shard_map/pallas_call | solution.py:41
  29.1 0.4 collective-permute-done.10.heard_ref
  29.5 0.0 collective-permute-done.9.got_ref
  29.5 0.1 shard_map.142
  29.6 15.8 %all_to_all.5.heard_ref = bf16[8,72,256]{2,1,0:T(8,128)(2,1)S(1)} all-to-all(bf16[8,72,256]{2,1,0:T(8,128)(2,1)S(1)} %shard_map.142), channel_id=1, replica_groups={{0,1,2,3,8,9,10,11},{4,5,6,7,12,13,14,15},{16,17,18,19,24,25,26,27},{20..., dimensions={0} | all-to-all | bytes 589824 | tf_op jit(solution)/shard_map/all_to_all | solution.py:349
  45.4 0.0 copy-done
  45.4 0.0 copy-done.1
  45.4 0.0 copy-done.2
  45.4 0.7 %shard_map.143 = (f32[64,256]{1,0:T(8,128)}, f32[64,256]{1,0:T(8,128)}, f32[64,256]{1,0:T(8,128)}, f32[64,256]{1,0:T(8,128)}, f32[1,128]{1,0:T(1,128)}) custom-call(bf16[8,72,256]{2,1,0:T(8,128)(2,1)S(1)} %all_to_all.5.heard_ref, f32[64,256]{1,0:T(8,128)S(1)} %copy-done, f32[64,256]{1,0:T(8,128)S(1)} %copy-done.1, f32[64,256]{1,0:T(8,128)S(1)} %copy-done.2), custom_call_target="tpu_custom_call" | custom-call | tf_op jit(solution)/shard_map/pallas_call | solution.py:41
  (7 shorter events, 0.0 us)
Async XLA Ops:
  1.8 10.9 %collective-permute-start.5 = (bf16[64,256]{1,0:T(8,128)(2,1)S(1)}, bf16[64,256]{1,0:T(8,128)(2,1)S(1)}, u32[]{:S(2)}, u32[]{:S(2)}) collective-permute-start(bf16[64,256]{1,0:T(8,128)(2,1)S(1)} %get-tuple-element.39), channel_id=1, source_target_pairs={{0,3},{1,0},{2,1},{3,2},{4,7},{5,4},{6,5},{7,6},{8,11},{9,8},{10,9... | collective-permute-start | bytes 98312 | tf_op jit(solution)/shard_map/ppermute | solution.py:329
  6.9 5.7 %collective-permute-start.4 = (bf16[64,256]{1,0:T(8,128)(2,1)S(1)}, bf16[64,256]{1,0:T(8,128)(2,1)S(1)}, u32[]{:S(2)}, u32[]{:S(2)}) collective-permute-start(bf16[64,256]{1,0:T(8,128)(2,1)S(1)} %get-tuple-element.39), channel_id=1, source_target_pairs={{0,2},{1,3},{2,0},{3,1},{4,6},{5,7},{6,4},{7,5},{8,10},{9,11},{10,... | collective-permute-start | bytes 98312 | tf_op jit(solution)/shard_map/ppermute | solution.py:329
  6.9 5.7 %collective-permute-start.3 = (bf16[64,256]{1,0:T(8,128)(2,1)S(1)}, bf16[64,256]{1,0:T(8,128)(2,1)S(1)}, u32[]{:S(2)}, u32[]{:S(2)}) collective-permute-start(bf16[64,256]{1,0:T(8,128)(2,1)S(1)} %get-tuple-element.39), channel_id=1, source_target_pairs={{0,1},{1,2},{2,3},{3,0},{4,5},{5,6},{6,7},{7,4},{8,9},{9,10},{10,1... | collective-permute-start | bytes 98312 | tf_op jit(solution)/shard_map/ppermute | solution.py:329
  7.9 12.8 %collective-permute-start.2 = (bf16[1024,128]{1,0:T(8,128)(2,1)S(1)}, bf16[1024,128]{1,0:T(8,128)(2,1)S(1)}, u32[]{:S(2)}, u32[]{:S(2)}) collective-permute-start(bf16[1024,128]{1,0:T(8,128)(2,1)S(1)} %get-tuple-element.30.refs_0_), channel_id=1, source_target_pairs={{0,4},{4,0},{8,12},{12,8},{1,5},{5,1},{9,13},{13,9},{2,6},{6,2},{1... | collective-permute-start | bytes 786440 | tf_op jit(solution)/shard_map/ppermute | solution.py:311
  7.9 9.2 %collective-permute-start = (bf16[1024,128]{1,0:T(8,128)(2,1)S(1)}, bf16[1024,128]{1,0:T(8,128)(2,1)S(1)}, u32[]{:S(2)}, u32[]{:S(2)}) collective-permute-start(bf16[1024,128]{1,0:T(8,128)(2,1)S(1)} %get-tuple-element.30.refs_0_), channel_id=1, source_target_pairs={{0,8},{4,12},{8,0},{12,4},{1,9},{5,13},{9,1},{13,5},{2,10},{6,14},... | collective-permute-start | bytes 786440 | tf_op jit(solution)/shard_map/ppermute | solution.py:311
  12.7 6.8 %collective-permute-start.6 = (bf16[256,256]{1,0:T(8,128)(2,1)S(1)}, bf16[256,256]{1,0:T(8,128)(2,1)S(1)}, u32[]{:S(2)}, u32[]{:S(2)}) collective-permute-start(bf16[256,256]{1,0:T(8,128)(2,1)S(1)} %constant_dynamic-update-slice_fusion.refs_0_), channel_id=1, source_target_pairs={{0,8},{4,12},{8,0},{12,4},{1,9},{5,13},{9,1},{13,5},{2,10},{6,14},... | collective-permute-start | bytes 393224 | tf_op jit(solution)/shard_map/ppermute | solution.py:311
  17.1 6.1 %collective-permute-start.1 = (bf16[1024,128]{1,0:T(8,128)(2,1)S(1)}, bf16[1024,128]{1,0:T(8,128)(2,1)S(1)}, u32[]{:S(2)}, u32[]{:S(2)}) collective-permute-start(bf16[1024,128]{1,0:T(8,128)(2,1)S(1)} %collective-permute-done.refs_0_), channel_id=1, source_target_pairs={{0,4},{4,0},{8,12},{12,8},{1,5},{5,1},{9,13},{13,9},{2,6},{6,2},{1... | collective-permute-start | bytes 786440 | tf_op jit(solution)/shard_map/ppermute | solution.py:311
  17.8 6.4 %collective-permute-start.7 = (bf16[256,256]{1,0:T(8,128)(2,1)S(1)}, bf16[256,256]{1,0:T(8,128)(2,1)S(1)}, u32[]{:S(2)}, u32[]{:S(2)}) collective-permute-start(bf16[256,256]{1,0:T(8,128)(2,1)S(1)} %constant_dynamic-update-slice_fusion.refs_0_), channel_id=1, source_target_pairs={{0,4},{4,0},{8,12},{12,8},{1,5},{5,1},{9,13},{13,9},{2,6},{6,2},{1... | collective-permute-start | bytes 393224 | tf_op jit(solution)/shard_map/ppermute | solution.py:311
  19.5 4.8 %collective-permute-start.8 = (bf16[256,256]{1,0:T(8,128)(2,1)S(1)}, bf16[256,256]{1,0:T(8,128)(2,1)S(1)}, u32[]{:S(2)}, u32[]{:S(2)}) collective-permute-start(bf16[256,256]{1,0:T(8,128)(2,1)S(1)} %collective-permute-done.6.refs_1_), channel_id=1, source_target_pairs={{0,4},{4,0},{8,12},{12,8},{1,5},{5,1},{9,13},{13,9},{2,6},{6,2},{1... | collective-permute-start | bytes 393224 | tf_op jit(solution)/shard_map/ppermute | solution.py:311
  27.4 2.1 %collective-permute-start.9 = (f32[512,256]{1,0:T(8,128)S(1)}, f32[512,256]{1,0:T(8,128)S(1)}, u32[]{:S(2)}, u32[]{:S(2)}) collective-permute-start(f32[512,256]{1,0:T(8,128)S(1)} %get-tuple-element.45), channel_id=1, source_target_pairs={{0,4},{4,0},{8,12},{12,8},{1,5},{5,1},{9,13},{13,9},{2,6},{6,2},{1... | collective-permute-start | bytes 1572872 | tf_op jit(solution)/shard_map/ppermute | solution.py:311
  28.0 1.5 %collective-permute-start.10 = (f32[8,128]{1,0:T(8,128)S(1)}, f32[8,128]{1,0:T(8,128)S(1)}, u32[]{:S(2)}, u32[]{:S(2)}) collective-permute-start(f32[8,128]{1,0:T(8,128)S(1)} %get-tuple-element.46.loss_ref), channel_id=1, source_target_pairs={{0,4},{4,0},{8,12},{12,8},{1,5},{5,1},{9,13},{13,9},{2,6},{6,2},{1... | collective-permute-start | bytes 12296 | tf_op jit(solution)/shard_map/ppermute | solution.py:311
  28.1 17.4 %copy-start = (f32[64,256]{1,0:T(8,128)S(1)}, f32[64,256]{1,0:T(8,128)}, u32[]{:S(2)}) copy-start(f32[64,256]{1,0:T(8,128)} %params_ref.1) | copy-start | bytes 196612
  28.1 17.4 %copy-start.1 = (f32[64,256]{1,0:T(8,128)S(1)}, f32[64,256]{1,0:T(8,128)}, u32[]{:S(2)}) copy-start(f32[64,256]{1,0:T(8,128)} %first_ref.1) | copy-start | bytes 196612
  28.1 17.4 %copy-start.2 = (f32[64,256]{1,0:T(8,128)S(1)}, f32[64,256]{1,0:T(8,128)}, u32[]{:S(2)}) copy-start(f32[64,256]{1,0:T(8,128)} %second_ref.1) | copy-start | bytes 196612
where the time goes:
time: 46.4 us; the launch traced here: 46.2 us
  blocking collectives  15.8 us (34%)
  Pallas kernels  10.8 us (23%)
  starting transfers between devices  10.4 us (22%)
  waiting for transfers between devices  6.34 us (14%)
  between operations  2.69 us (6%)
    all_to_all x1, blocking collectives, body(): lax.all_to_all(sent, ('keys', 'qry'), 0, 0, axis_index_groups=groups, til...  15.8 us
    pallas_call x8, Pallas kernels, call(): pl.pallas_call(kernel, out_shape=shapes, in_specs=[sm] * len(scalars) + [...  9.65 us
    ppermute x3, starting transfers between devices, body(): lax.ppermute(copies, 'qry', [(i, (i + d) % n_qry) for i in range(n_qry)])  6.14 us
    ppermute x8, starting transfers between devices, swap(): return lax.ppermute(block, 'keys', [(k, k ^ bit) for k in range(n_keys)])  4.25 us
    ppermute x8, waiting for transfers between devices, swap(): return lax.ppermute(block, 'keys', [(k, k ^ bit) for k in range(n_keys)])  3.78 us
    ppermute x3, waiting for transfers between devices, body(): lax.ppermute(copies, 'qry', [(i, (i + d) % n_qry) for i in range(n_qry)])  2.56 us
    pallas_call x1, Pallas kernels, load(): pl.pallas_call(kernel, out_shape=(pltpu.VMEM(slot_params.shape, jnp.bfloa...  1.15 us
  transfers between devices with their start and end apart: 11, of which 4 were waited for; matrix products, arithmetic and copies ran while one was open for 0% of the time, Pallas kernels for 12%

commit v1 on v0

--- a/solution.py
+++ b/solution.py
@@ -11,6 +11,7 @@
 NEG = -1e30
 PAD = 8
 LANES = 128
+TILE = 128
 GRANT = 24 * 2**20
 
 
@@ -27,25 +28,29 @@
     return jnp.concatenate([turned, jnp.ones((PAD, turned.shape[1]), turned.dtype)], axis=0)
 
 
+def fold(block, join):
+    groups = [block[r:r + PAD] for r in range(0, block.shape[0], PAD)]
+    while len(groups) > 1:
+        groups = [join(*groups[g:g + 2]) if g + 1 < len(groups) else groups[g] for g in range(0, len(groups), 2)]
+    return groups[0]
+
+
 def row_block(rows):
     return math.gcd(rows, 256)
 
 
-def call(kernel, out, scalars, arrays, scratch=(), hbm_out=()):
-    vm = pl.BlockSpec(memory_space=pltpu.VMEM)
-    sm = pl.BlockSpec(memory_space=pltpu.SMEM)
+def call(kernel, out, arrays, scratch=(), hbm_out=()):
+    vm, hbm = pl.BlockSpec(memory_space=pltpu.VMEM), pl.BlockSpec(memory_space=pltpu.HBM)
     arrays = [pltpu.with_memory_space_constraint(a, pltpu.VMEM) for a in arrays]
-    shapes = tuple(
-        jax.ShapeDtypeStruct(s, d) if i in hbm_out else pltpu.VMEM(s, d) for i, (s, d) in enumerate(out)
-    )
+    spaces = [pltpu.HBM if i in hbm_out else pltpu.VMEM for i in range(len(out))]
     return pl.pallas_call(
         kernel,
-        out_shape=shapes,
-        in_specs=[sm] * len(scalars) + [vm] * len(arrays),
-        out_specs=tuple(vm for _ in shapes),
+        out_shape=tuple(space(s, d) for space, (s, d) in zip(spaces, out)),
+        in_specs=[vm] * len(arrays),
+        out_specs=tuple(hbm if i in hbm_out else vm for i in range(len(out))),
         scratch_shapes=list(scratch),
         compiler_params=pltpu.CompilerParams(vmem_limit_bytes=GRANT),
-    )(*scalars, *arrays)
+    )(*arrays)
 
 
 def load(queries, keys, values, slot_params):
@@ -118,9 +123,12 @@
                     lax.broadcasted_iota(jnp.int32, turned.shape, 1) < count, turned, jnp.zeros_like(turned)
                 )
                 for at in blocks:
-                    score = nt(keys, q_ref[at, :])
-                    score_ref[:, at] = score
-                    peak_ref[:, at] = jnp.max(score, axis=0, keepdims=True)
+                    peak = jnp.full((PAD, step), NEG, jnp.float32)
+                    for t in range(0, size, TILE):
+                        score = nt(keys[t:t + TILE], q_ref[at, :])
+                        score_ref[t:t + TILE, at] = score
+                        peak = jnp.maximum(peak, fold(score, jnp.maximum))
+                    peak_ref[:, at] = jnp.max(peak, axis=0, keepdims=True)
                 for at in blocks:
                     big = big_ref[:, at]
                     new_big = jnp.maximum(big, peak_ref[:, at])
@@ -142,10 +150,7 @@
     scratch += [
         pltpu.VMEM((segments[0][1].shape[0] // 2, rows), jnp.float32), pltpu.VMEM((1, rows), jnp.float32)
     ]
-    return call(
-        kernel, ends if last else shapes, [], [live] + arrays, scratch,
-        hbm_out=(0,) if last else (),
-    )
+    return call(kernel, ends if last else shapes, [live] + arrays, scratch)
 
 
 def gradient_half(start, half, q_ref, prob_ref, cast_ref, diff_ref, inner_ref, values_ref, grad_ref, dscore_ref, scale):
@@ -222,21 +227,29 @@
             ((count, width), jnp.bfloat16),
             ((PAD, LANES), jnp.float32),
         ],
-        [], [queries, teach, *slots, *other],
+        [queries, teach, *slots, *other],
         [pltpu.VMEM((count, width), jnp.bfloat16), pltpu.VMEM((half, rows), jnp.bfloat16)],
     )
 
 
-def own_half(queries, prob, cast, diff, inner, values, half, scale):
-    def kernel(*refs):
+def own_half(queries, teach_rows, prob, cast, diff, inner, values, half, scale):
+    rows, width = queries.shape
+
+    def kernel(rows_ref, q_ref, prob_ref, cast_ref, diff_ref, inner_ref, values_ref, *refs):
+        grad_ref, out_ref, dscore_ref, sem = refs
+        write = pltpu.make_async_copy(rows_ref, out_ref, sem)
+        write.start()
         start = pl.multiple_of(lax.rem(lax.axis_index("keys"), 2) * half, half)
-        gradient_half(start, half, *refs, scale)
+        gradient_half(
+            start, half, q_ref, prob_ref, cast_ref, diff_ref, inner_ref, values_ref, grad_ref, dscore_ref, scale
+        )
+        write.wait()
 
     return call(
-        kernel, [((half, 2 * queries.shape[1]), jnp.float32)],
-        [], [queries, prob, cast, diff, inner, values],
-        [pltpu.VMEM((half, queries.shape[0]), jnp.bfloat16)],
-    )[0]
+        kernel, [((half, 2 * width), jnp.float32), ((rows, width), jnp.bfloat16)],
+        [teach_rows, queries, prob, cast, diff, inner, values],
+        [pltpu.VMEM((half, rows), jnp.bfloat16), pltpu.SemaphoreType.DMA(())], hbm_out=(1,),
+    )
 
 
 def packed(own, got, loss, heard, per):
@@ -261,30 +274,39 @@
             for at in range(0, wide, LANES):
                 out_ref[b, per:, pl.ds(at, LANES)] = parts
 
-    return call(kernel, [((blocks, per + PAD, wide), jnp.bfloat16)], [], [own, got, loss, heard])[0]
+    return call(kernel, [((blocks, per + PAD, wide), jnp.bfloat16)], [own, got, loss, heard])[0]
 
 
 def update(heard, slot_params, first_moment, second_moment, terms):
     per, wide = slot_params.shape
 
-    def kernel(heard_ref, params_ref, first_ref, second_ref, grad_ref, p_ref, f_ref, s_ref, loss_ref):
+    def kernel(heard_ref, params_ref, first_ref, second_ref, *refs):
+        outs, bufs, sems = refs[:5], refs[5:10], refs[10]
+        moves = [pltpu.make_async_copy(b, o, sems.at[i]) for i, (b, o) in enumerate(zip(bufs, outs))]
         grad = jnp.zeros((per, wide), jnp.float32)
         tail = jnp.zeros((PAD, LANES), jnp.float32)
         for b in range(heard_ref.shape[0]):
             grad = grad + heard_ref[b, :per, :].astype(jnp.float32)
             tail = tail + heard_ref[b, per:, :LANES].astype(jnp.float32)
-        grad_ref[...] = grad
+        bufs[0][...] = grad
+        moves[0].start()
         new_first = 0.9 * first_ref[...] + 0.1 * grad
+        bufs[2][...] = new_first
+        moves[2].start()
         new_second = 0.95 * second_ref[...] + 0.05 * grad * grad
-        f_ref[...] = new_first
-        s_ref[...] = new_second
-        p_ref[...] = params_ref[...] - 0.02 * new_first / (jnp.sqrt(new_second) + 1e-08)
-        loss_ref[...] = jnp.sum(tail, axis=0, keepdims=True) / terms
-
-    shape = ((per, wide), jnp.float32)
+        bufs[3][...] = new_second
+        moves[3].start()
+        bufs[4][...] = jnp.sum(tail, axis=0, keepdims=True) / terms
+        moves[4].start()
+        bufs[1][...] = params_ref[...] - 0.02 * new_first / (jnp.sqrt(new_second) + 1e-08)
+        moves[1].start()
+        for move in moves:
+            move.wait()
+
+    outs = [((per, wide), jnp.float32)] * 4 + [((1, LANES), jnp.float32)]
     return call(
-        kernel, [shape] * 4 + [((1, LANES), jnp.float32)], [],
-        [heard, slot_params, first_moment, second_moment], hbm_out=(0, 1, 2, 3, 4),
+        kernel, outs, [heard, slot_params, first_moment, second_moment],
+        [pltpu.VMEM(s, d) for s, d in outs] + [pltpu.SemaphoreType.DMA((5,))], hbm_out=(0, 1, 2, 3, 4),
     )
 
 
@@ -342,7 +364,7 @@
     teacher_rows, teacher_turned = state
 
     away, prob, cast, diff, inner, values, loss = student(flat, teacher_turned, slots, other, per, half, scale)
-    own = own_half(flat, prob, cast, diff, inner, values, half, scale)
+    own, teacher_out = own_half(flat, teacher_rows, prob, cast, diff, inner, values, half, scale)
     sent = packed(own, swap(away, 1), loss, swap(loss, 1), per)
 
     groups = [[(2 * x + c) * n_qry + q for x in range(n_chip) for q in range(n_qry)] for c in range(2)]
@@ -350,7 +372,7 @@
     slot_grad, new_params, new_first, new_second, loss = update(
         heard, slot_params, first_moment, second_moment, rows * n_keys * n_qry
     )
-    teacher_out = teacher_rows.reshape(tok, heads, width)
+    teacher_out = teacher_out.reshape(tok, heads, width)
     return (teacher_out, slot_grad, new_params, new_first, new_second, loss[0, :1])
 
 

time: 46.4 us -> 45.6 us (0.983)
  Pallas kernels: 10.8 us -> 9.93 us
    pallas_call x8, Pallas kernels: 9.65 us -> 8.78 us  [call(): pl.pallas_call(kernel, out_shape=tuple((space(s, d) for space, (s, d) in...]
  transfers between devices with their start and end apart: 11 -> 11, of which waited for: 4 -> 4; matrix products, arithmetic and copies ran while one was open for 0% -> 0% of each run, Pallas kernels for 12% -> 10%
where the time goes in v1:
time: 45.6 us; the launch traced here: 45.4 us
  blocking collectives  15.8 us (35%)
  starting transfers between devices  10.4 us (23%)
  Pallas kernels  9.93 us (22%)
  waiting for transfers between devices  6.32 us (14%)
  between operations  2.72 us (6%)
    all_to_all x1, blocking collectives, body(): lax.all_to_all(sent, ('keys', 'qry'), 0, 0, axis_index_groups=groups, til...  15.8 us
    pallas_call x8, Pallas kernels, call(): pl.pallas_call(kernel, out_shape=tuple((space(s, d) for space, (s, d) in...  8.78 us
    ppermute x3, starting transfers between devices, body(): lax.ppermute(copies, 'qry', [(i, (i + d) % n_qry) for i in range(n_qry)])  6.14 us
    ppermute x8, starting transfers between devices, swap(): return lax.ppermute(block, 'keys', [(k, k ^ bit) for k in range(n_keys)])  4.28 us
    ppermute x8, waiting for transfers between devices, swap(): return lax.ppermute(block, 'keys', [(k, k ^ bit) for k in range(n_keys)])  3.77 us
    ppermute x3, waiting for transfers between devices, body(): lax.ppermute(copies, 'qry', [(i, (i + d) % n_qry) for i in range(n_qry)])  2.56 us
    pallas_call x1, Pallas kernels, load(): pl.pallas_call(kernel, out_shape=(pltpu.VMEM(slot_params.shape, jnp.bfloa...  1.15 us
  transfers between devices with their start and end apart: 11, of which 4 were waited for; matrix products, arithmetic and copies ran while one was open for 0% of the time, Pallas kernels for 10%

profile of v1, /device:TPU:0, one launch (start us, length us, event | category | flops | bytes accessed | tf_op | source)
XLA Modules:
  0.0 45.4 jit_solution(3825027553535803514)
XLA Ops:
  0.6 1.2 %load.1 = (bf16[64,256]{1,0:T(8,128)(2,1)S(1)}, bf16[1024,128]{1,0:T(8,128)(2,1)S(1)}, bf16[1024,128]{1,0:T(8,128)(2,1)S(1)}) custom-call(f32[64,256]{1,0:T(8,128)} %params_ref.1, bf16[512,128]{1,0:T(8,128)(2,1)} %refs_1_.1, bf16[512,128]{1,0:T(8,128)(2,1)} %refs_2_.1, bf16[1024,128]{1,0:T(8,128)(2,1)} %bitcast.10), custom_call_target="tpu_custom_call" | custom-call | tf_op jit(solution)/shard_map/load/pallas_call | solution.py:71
  1.8 5.1 %collective-permute-start.5 = (bf16[64,256]{1,0:T(8,128)(2,1)S(1)}, bf16[64,256]{1,0:T(8,128)(2,1)S(1)}, u32[]{:S(2)}, u32[]{:S(2)}) collective-permute-start(bf16[64,256]{1,0:T(8,128)(2,1)S(1)} %get-tuple-element.41), channel_id=1, source_target_pairs={{0,3},{1,0},{2,1},{3,2},{4,7},{5,4},{6,5},{7,6},{8,11},{9,8},{10,9... | collective-permute-start | bytes 98312 | tf_op jit(solution)/shard_map/ppermute | solution.py:351
  6.9 0.0 collective-permute-start.4
  6.9 1.0 %collective-permute-start.3 = (bf16[64,256]{1,0:T(8,128)(2,1)S(1)}, bf16[64,256]{1,0:T(8,128)(2,1)S(1)}, u32[]{:S(2)}, u32[]{:S(2)}) collective-permute-start(bf16[64,256]{1,0:T(8,128)(2,1)S(1)} %get-tuple-element.41), channel_id=1, source_target_pairs={{0,1},{1,2},{2,3},{3,0},{4,5},{5,6},{6,7},{7,4},{8,9},{9,10},{10,1... | collective-permute-start | bytes 98312 | tf_op jit(solution)/shard_map/ppermute | solution.py:351
  7.9 0.0 collective-permute-start.2
  7.9 1.5 %collective-permute-start = (bf16[1024,128]{1,0:T(8,128)(2,1)S(1)}, bf16[1024,128]{1,0:T(8,128)(2,1)S(1)}, u32[]{:S(2)}, u32[]{:S(2)}) collective-permute-start(bf16[1024,128]{1,0:T(8,128)(2,1)S(1)} %get-tuple-element.32.refs_0_), channel_id=1, source_target_pairs={{0,8},{4,12},{8,0},{12,4},{1,9},{5,13},{9,1},{13,5},{2,10},{6,14},... | collective-permute-start | bytes 786440 | tf_op jit(solution)/shard_map/ppermute | solution.py:333
  10.1 2.6 %collective-permute-done.3 = bf16[64,256]{1,0:T(8,128)(2,1)S(1)} collective-permute-done((bf16[64,256]{1,0:T(8,128)(2,1)S(1)}, bf16[64,256]{1,0:T(8,128)(2,1)S(1)}, u32[]{:S(2)}, u32[]{:S(2)}) %collective-permute-start.3) | collective-permute-done | bytes 32800 | tf_op jit(solution)/shard_map/ppermute | solution.py:351
  12.6 0.0 collective-permute-done.4
  12.7 0.0 collective-permute-done.5
  12.7 1.6 %collective-permute-start.6 = (bf16[256,256]{1,0:T(8,128)(2,1)S(1)}, bf16[256,256]{1,0:T(8,128)(2,1)S(1)}, u32[]{:S(2)}, u32[]{:S(2)}) collective-permute-start(bf16[256,256]{1,0:T(8,128)(2,1)S(1)} %constant_dynamic-update-slice_fusion.refs_0_), channel_id=1, source_target_pairs={{0,8},{4,12},{8,0},{12,4},{1,9},{5,13},{9,1},{13,5},{2,10},{6,14},... | collective-permute-start | bytes 393224 | tf_op jit(solution)/shard_map/ppermute | solution.py:333
  14.9 2.2 %collective-permute-done.refs_0_ = bf16[1024,128]{1,0:T(8,128)(2,1)S(1)} collective-permute-done((bf16[1024,128]{1,0:T(8,128)(2,1)S(1)}, bf16[1024,128]{1,0:T(8,128)(2,1)S(1)}, u32[]{:S(2)}, u32[]{:S(2)}) %collective-permute-start) | collective-permute-done | bytes 262176 | tf_op jit(solution)/shard_map/ppermute | solution.py:333
  17.1 0.0 collective-permute-start.1
  17.8 0.6 %collective-permute-start.7 = (bf16[256,256]{1,0:T(8,128)(2,1)S(1)}, bf16[256,256]{1,0:T(8,128)(2,1)S(1)}, u32[]{:S(2)}, u32[]{:S(2)}) collective-permute-start(bf16[256,256]{1,0:T(8,128)(2,1)S(1)} %constant_dynamic-update-slice_fusion.refs_0_), channel_id=1, source_target_pairs={{0,4},{4,0},{8,12},{12,8},{1,5},{5,1},{9,13},{13,9},{2,6},{6,2},{1... | collective-permute-start | bytes 393224 | tf_op jit(solution)/shard_map/ppermute | solution.py:333
  18.4 1.1 %collective-permute-done.6.refs_1_ = bf16[256,256]{1,0:T(8,128)(2,1)S(1)} collective-permute-done((bf16[256,256]{1,0:T(8,128)(2,1)S(1)}, bf16[256,256]{1,0:T(8,128)(2,1)S(1)}, u32[]{:S(2)}, u32[]{:S(2)}) %collective-permute-start.6) | collective-permute-done | bytes 131104 | tf_op jit(solution)/shard_map/ppermute | solution.py:333
  19.5 0.0 collective-permute-start.8
  19.5 0.1 fusion.1.live_ref
  19.5 1.1 %shard_map.136 = (f32[1,1024]{1,0:T(1,128)S(1)}, f32[136,1024]{1,0:T(8,128)S(1)}) custom-call(s32[8,128]{1,0:T(8,128)S(1)} %fusion.1.live_ref, bf16[1024,128]{1,0:T(8,128)(2,1)S(1)} %get-tuple-element.31.q_ref, bf16[1024,128]{1,0:T(8,128)(2,1)S(1)} %get-tuple-element.32.refs_0_), custom_call_target="tpu_custom_call" | custom-call | tf_op jit(solution)/shard_map/pallas_call | solution.py:46
  20.7 0.0 collective-permute-done.2.refs_0_
  20.7 1.1 %shard_map.137 = (f32[1,1024]{1,0:T(1,128)S(1)}, f32[136,1024]{1,0:T(8,128)S(1)}) custom-call(s32[8,128]{1,0:T(8,128)S(1)} %fusion.1.live_ref, bf16[1024,128]{1,0:T(8,128)(2,1)S(1)} %get-tuple-element.31.q_ref, bf16[1024,128]{1,0:T(8,128)(2,1)S(1)} %collective-permute-done.2.refs_0_, f32[1,1024]{1,0:T(1,128)S(1)} %get-tuple-element.33.refs_1_, ...), custom_call_target="tpu_custom_call" | custom-call | tf_op jit(solution)/shard_map/pallas_call | solution.py:46
  21.8 1.1 %shard_map.138 = (f32[1,1024]{1,0:T(1,128)S(1)}, f32[136,1024]{1,0:T(8,128)S(1)}) custom-call(s32[8,128]{1,0:T(8,128)S(1)} %fusion.1.live_ref, bf16[1024,128]{1,0:T(8,128)(2,1)S(1)} %get-tuple-element.31.q_ref, bf16[1024,128]{1,0:T(8,128)(2,1)S(1)} %collective-permute-done.refs_0_, f32[1,1024]{1,0:T(1,128)S(1)} %get-tuple-element.35.refs_1_, ...), custom_call_target="tpu_custom_call" | custom-call | tf_op jit(solution)/shard_map/pallas_call | solution.py:46
  23.0 0.0 collective-permute-done.1.refs_0_
  23.0 0.3 shard_map.139
  23.3 0.0 collective-permute-done.7.refs_2_
  23.3 0.0 collective-permute-done.8.refs_3_
  23.3 3.2 %shard_map.140 = (f32[512,256]{1,0:T(8,128)S(1)}, f32[1024,1024]{1,0:T(8,128)S(1)}, bf16[1024,1024]{1,0:T(8,128)(2,1)S(1)}, bf16[1024,128]{1,0:T(8,128)(2,1)S(1)...) custom-call(bf16[1024,128]{1,0:T(8,128)(2,1)S(1)} %get-tuple-element.31.q_ref, ...), custom_call_target="tpu_custom_call" | custom-call | tf_op jit(solution)/shard_map/pallas_call | solution.py:46
  26.5 0.6 %collective-permute-start.9 = (f32[512,256]{1,0:T(8,128)S(1)}, f32[512,256]{1,0:T(8,128)S(1)}, u32[]{:S(2)}, u32[]{:S(2)}) collective-permute-start(f32[512,256]{1,0:T(8,128)S(1)} %get-tuple-element.49), channel_id=1, source_target_pairs={{0,4},{4,0},{8,12},{12,8},{1,5},{5,1},{9,13},{13,9},{2,6},{6,2},{1... | collective-permute-start | bytes 1572872 | tf_op jit(solution)/shard_map/ppermute | solution.py:333
  27.1 0.1 collective-permute-start.10
  27.2 0.0 copy-start
  27.2 0.0 copy-start.1
  27.2 0.0 copy-start.2
  27.2 1.0 %shard_map.141 = (f32[512,256]{1,0:T(8,128)S(1)}, bf16[1024,128]{1,0:T(8,128)(2,1)}) custom-call(bf16[1024,128]{1,0:T(8,128)(2,1)S(1)} %get-tuple-element.39.rows_ref, bf16[1024,128]{1,0:T(8,128)(2,1)S(1)} %get-tuple-element.31.q_ref, f32[1024,1024]{1,0:T(8,128)S(1)} %get-tuple-element.42.prob_ref, bf16[1024,1024]{1,0:T(8,128)(2,1)S(1)} %get-tuple-element.43.cast_ref, ...), custom_call_target="tpu_custom_call" | custom-call | tf_op jit(solution)/shard_map/pallas_call | solution.py:46
  28.2 0.4 collective-permute-done.10.heard_ref
  28.7 0.0 collective-permute-done.9.got_ref
  28.7 0.1 shard_map.142
  28.7 15.8 %all_to_all.5.heard_ref = bf16[8,72,256]{2,1,0:T(8,128)(2,1)S(1)} all-to-all(bf16[8,72,256]{2,1,0:T(8,128)(2,1)S(1)} %shard_map.142), channel_id=1, replica_groups={{0,1,2,3,8,9,10,11},{4,5,6,7,12,13,14,15},{16,17,18,19,24,25,26,27},{20..., dimensions={0} | all-to-all | bytes 589824 | tf_op jit(solution)/shard_map/all_to_all | solution.py:371
  44.5 0.0 copy-done
  44.5 0.0 copy-done.1
  44.6 0.0 copy-done.2
  44.6 0.8 %shard_map.143 = (f32[64,256]{1,0:T(8,128)}, f32[64,256]{1,0:T(8,128)}, f32[64,256]{1,0:T(8,128)}, f32[64,256]{1,0:T(8,128)}, f32[1,128]{1,0:T(1,128)}) custom-call(bf16[8,72,256]{2,1,0:T(8,128)(2,1)S(1)} %all_to_all.5.heard_ref, f32[64,256]{1,0:T(8,128)S(1)} %copy-done, f32[64,256]{1,0:T(8,128)S(1)} %copy-done.1, f32[64,256]{1,0:T(8,128)S(1)} %copy-done.2), custom_call_target="tpu_custom_call" | custom-call | tf_op jit(solution)/shard_map/pallas_call | solution.py:46
  (7 shorter events, 0.0 us)
Async XLA Ops:
  1.8 10.9 %collective-permute-start.5 = (bf16[64,256]{1,0:T(8,128)(2,1)S(1)}, bf16[64,256]{1,0:T(8,128)(2,1)S(1)}, u32[]{:S(2)}, u32[]{:S(2)}) collective-permute-start(bf16[64,256]{1,0:T(8,128)(2,1)S(1)} %get-tuple-element.41), channel_id=1, source_target_pairs={{0,3},{1,0},{2,1},{3,2},{4,7},{5,4},{6,5},{7,6},{8,11},{9,8},{10,9... | collective-permute-start | bytes 98312 | tf_op jit(solution)/shard_map/ppermute | solution.py:351
  6.9 5.7 %collective-permute-start.4 = (bf16[64,256]{1,0:T(8,128)(2,1)S(1)}, bf16[64,256]{1,0:T(8,128)(2,1)S(1)}, u32[]{:S(2)}, u32[]{:S(2)}) collective-permute-start(bf16[64,256]{1,0:T(8,128)(2,1)S(1)} %get-tuple-element.41), channel_id=1, source_target_pairs={{0,2},{1,3},{2,0},{3,1},{4,6},{5,7},{6,4},{7,5},{8,10},{9,11},{10,... | collective-permute-start | bytes 98312 | tf_op jit(solution)/shard_map/ppermute | solution.py:351
  6.9 5.7 %collective-permute-start.3 = (bf16[64,256]{1,0:T(8,128)(2,1)S(1)}, bf16[64,256]{1,0:T(8,128)(2,1)S(1)}, u32[]{:S(2)}, u32[]{:S(2)}) collective-permute-start(bf16[64,256]{1,0:T(8,128)(2,1)S(1)} %get-tuple-element.41), channel_id=1, source_target_pairs={{0,1},{1,2},{2,3},{3,0},{4,5},{5,6},{6,7},{7,4},{8,9},{9,10},{10,1... | collective-permute-start | bytes 98312 | tf_op jit(solution)/shard_map/ppermute | solution.py:351
  7.9 12.8 %collective-permute-start.2 = (bf16[1024,128]{1,0:T(8,128)(2,1)S(1)}, bf16[1024,128]{1,0:T(8,128)(2,1)S(1)}, u32[]{:S(2)}, u32[]{:S(2)}) collective-permute-start(bf16[1024,128]{1,0:T(8,128)(2,1)S(1)} %get-tuple-element.32.refs_0_), channel_id=1, source_target_pairs={{0,4},{4,0},{8,12},{12,8},{1,5},{5,1},{9,13},{13,9},{2,6},{6,2},{1... | collective-permute-start | bytes 786440 | tf_op jit(solution)/shard_map/ppermute | solution.py:333
  7.9 9.2 %collective-permute-start = (bf16[1024,128]{1,0:T(8,128)(2,1)S(1)}, bf16[1024,128]{1,0:T(8,128)(2,1)S(1)}, u32[]{:S(2)}, u32[]{:S(2)}) collective-permute-start(bf16[1024,128]{1,0:T(8,128)(2,1)S(1)} %get-tuple-element.32.refs_0_), channel_id=1, source_target_pairs={{0,8},{4,12},{8,0},{12,4},{1,9},{5,13},{9,1},{13,5},{2,10},{6,14},... | collective-permute-start | bytes 786440 | tf_op jit(solution)/shard_map/ppermute | solution.py:333
  12.7 6.8 %collective-permute-start.6 = (bf16[256,256]{1,0:T(8,128)(2,1)S(1)}, bf16[256,256]{1,0:T(8,128)(2,1)S(1)}, u32[]{:S(2)}, u32[]{:S(2)}) collective-permute-start(bf16[256,256]{1,0:T(8,128)(2,1)S(1)} %constant_dynamic-update-slice_fusion.refs_0_), channel_id=1, source_target_pairs={{0,8},{4,12},{8,0},{12,4},{1,9},{5,13},{9,1},{13,5},{2,10},{6,14},... | collective-permute-start | bytes 393224 | tf_op jit(solution)/shard_map/ppermute | solution.py:333
  17.1 5.8 %collective-permute-start.1 = (bf16[1024,128]{1,0:T(8,128)(2,1)S(1)}, bf16[1024,128]{1,0:T(8,128)(2,1)S(1)}, u32[]{:S(2)}, u32[]{:S(2)}) collective-permute-start(bf16[1024,128]{1,0:T(8,128)(2,1)S(1)} %collective-permute-done.refs_0_), channel_id=1, source_target_pairs={{0,4},{4,0},{8,12},{12,8},{1,5},{5,1},{9,13},{13,9},{2,6},{6,2},{1... | collective-permute-start | bytes 786440 | tf_op jit(solution)/shard_map/ppermute | solution.py:333
  17.8 5.5 %collective-permute-start.7 = (bf16[256,256]{1,0:T(8,128)(2,1)S(1)}, bf16[256,256]{1,0:T(8,128)(2,1)S(1)}, u32[]{:S(2)}, u32[]{:S(2)}) collective-permute-start(bf16[256,256]{1,0:T(8,128)(2,1)S(1)} %constant_dynamic-update-slice_fusion.refs_0_), channel_id=1, source_target_pairs={{0,4},{4,0},{8,12},{12,8},{1,5},{5,1},{9,13},{13,9},{2,6},{6,2},{1... | collective-permute-start | bytes 393224 | tf_op jit(solution)/shard_map/ppermute | solution.py:333
  19.5 3.9 %collective-permute-start.8 = (bf16[256,256]{1,0:T(8,128)(2,1)S(1)}, bf16[256,256]{1,0:T(8,128)(2,1)S(1)}, u32[]{:S(2)}, u32[]{:S(2)}) collective-permute-start(bf16[256,256]{1,0:T(8,128)(2,1)S(1)} %collective-permute-done.6.refs_1_), channel_id=1, source_target_pairs={{0,4},{4,0},{8,12},{12,8},{1,5},{5,1},{9,13},{13,9},{2,6},{6,2},{1... | collective-permute-start | bytes 393224 | tf_op jit(solution)/shard_map/ppermute | solution.py:333
  26.5 2.1 %collective-permute-start.9 = (f32[512,256]{1,0:T(8,128)S(1)}, f32[512,256]{1,0:T(8,128)S(1)}, u32[]{:S(2)}, u32[]{:S(2)}) collective-permute-start(f32[512,256]{1,0:T(8,128)S(1)} %get-tuple-element.49), channel_id=1, source_target_pairs={{0,4},{4,0},{8,12},{12,8},{1,5},{5,1},{9,13},{13,9},{2,6},{6,2},{1... | collective-permute-start | bytes 1572872 | tf_op jit(solution)/shard_map/ppermute | solution.py:333
  27.1 1.5 %collective-permute-start.10 = (f32[8,128]{1,0:T(8,128)S(1)}, f32[8,128]{1,0:T(8,128)S(1)}, u32[]{:S(2)}, u32[]{:S(2)}) collective-permute-start(f32[8,128]{1,0:T(8,128)S(1)} %get-tuple-element.50.loss_ref), channel_id=1, source_target_pairs={{0,4},{4,0},{8,12},{12,8},{1,5},{5,1},{9,13},{13,9},{2,6},{6,2},{1... | collective-permute-start | bytes 12296 | tf_op jit(solution)/shard_map/ppermute | solution.py:333
  27.2 17.4 %copy-start = (f32[64,256]{1,0:T(8,128)S(1)}, f32[64,256]{1,0:T(8,128)}, u32[]{:S(2)}) copy-start(f32[64,256]{1,0:T(8,128)} %params_ref.1) | copy-start | bytes 196612
  27.2 17.4 %copy-start.1 = (f32[64,256]{1,0:T(8,128)S(1)}, f32[64,256]{1,0:T(8,128)}, u32[]{:S(2)}) copy-start(f32[64,256]{1,0:T(8,128)} %first_ref.1) | copy-start | bytes 196612
  27.2 17.4 %copy-start.2 = (f32[64,256]{1,0:T(8,128)S(1)}, f32[64,256]{1,0:T(8,128)}, u32[]{:S(2)}) copy-start(f32[64,256]{1,0:T(8,128)} %second_ref.1) | copy-start | bytes 196612

commit v2 on v1

--- a/solution.py
+++ b/solution.py
@@ -33,6 +33,12 @@
     while len(groups) > 1:
         groups = [join(*groups[g:g + 2]) if g + 1 < len(groups) else groups[g] for g in range(0, len(groups), 2)]
     return groups[0]
+
+
+def peer(index, d, count):
+    if count & (count - 1):
+        return (index - d + count) % count if isinstance(index, int) else lax.rem(index - d + count, count)
+    return index ^ d
 
 
 def row_block(rows):
@@ -112,6 +118,7 @@
         for s, offset in enumerate(offsets):
             cache_ref = seg[s]
             size = cache_ref.shape[0] // 2
+            tile = math.gcd(size, TILE)
             count = jnp.max(live_ref[offset:offset + 1, :])
 
             @pl.when(count > 0)
@@ -124,9 +131,9 @@
                 )
                 for at in blocks:
                     peak = jnp.full((PAD, step), NEG, jnp.float32)
-                    for t in range(0, size, TILE):
-                        score = nt(keys[t:t + TILE], q_ref[at, :])
-                        score_ref[t:t + TILE, at] = score
+                    for t in range(0, size, tile):
+                        score = nt(keys[t:t + tile], q_ref[at, :])
+                        score_ref[t:t + tile, at] = score
                         peak = jnp.maximum(peak, fold(score, jnp.maximum))
                     peak_ref[:, at] = jnp.max(peak, axis=0, keepdims=True)
                 for at in blocks:
@@ -161,8 +168,8 @@
         at = pl.ds(at, step)
         slope = nt(values, diff_ref[at, :]) - inner_ref[:, at]
         dscore_ref[:, at] = (prob_ref[pl.ds(start, half), at] * slope).astype(jnp.bfloat16)
-    grad_ref[:, width:] = nn(cast_ref[pl.ds(start, half), :], diff_ref[...])
-    grad_ref[:, :width] = nn(dscore_ref[...], q_ref[...]) * scale
+    grad_ref[:half, width:] = nn(cast_ref[pl.ds(start, half), :], diff_ref[...])
+    grad_ref[:half, :width] = nn(dscore_ref[...], q_ref[...]) * scale
 
 
 def student(queries, teach, slots, other, per, half, scale):
@@ -171,18 +178,19 @@
     step = row_block(rows)
     pieces = slots[0].shape[0] // per
     count = 2 * rounds * pieces * per
+    tile = math.gcd(count, TILE)
     factor = scale * math.log2(math.e)
 
     def kernel(q_ref, teach_ref, *refs):
         sources, refs = refs[: 2 * rounds], refs[2 * rounds:]
-        grad_ref, prob_ref, cast_ref, diff_ref, inner_ref, values_ref, loss_ref, keys_ref, dscore_ref = refs
+        grad_ref, prob_ref, cast_ref, diff_ref, inner_ref, values_ref, keys_ref, dscore_ref = refs
         n_chip, n_qry = lax.axis_size("keys") // 2, lax.axis_size("qry")
         me, mine = lax.axis_index("keys"), lax.axis_index("qry")
         core, chip = lax.rem(me, 2), lax.div(me, 2)
         for r, source in enumerate(sources):
             c, x = (core, r) if r < rounds else (1 - core, r - rounds)
             for d in range(pieces):
-                place = (c * n_chip + (chip ^ x)) * n_qry + lax.rem(mine - d + n_qry, n_qry)
+                place = (c * n_chip + (chip ^ x)) * n_qry + peer(mine, d, n_qry)
                 to = pl.multiple_of(place * per, per)
                 piece = source[pl.ds(d * per, per), :]
                 keys_ref[pl.ds(to, per), :] = piece[:, :width]
@@ -191,13 +199,19 @@
         squares = jnp.zeros((width, step), jnp.float32)
         blocks = [pl.ds(at, step) for at in range(0, rows, step)]
         for at in blocks:
-            score = nt(keys_ref[...], q_ref[at, :])
-            prob_ref[:, at] = score
-            inner_ref[:, at] = jnp.max(score, axis=0, keepdims=True)
+            peak = jnp.full((PAD, step), NEG, jnp.float32)
+            for t in range(0, count, tile):
+                score = nt(keys_ref[t:t + tile, :], q_ref[at, :])
+                prob_ref[t:t + tile, at] = score
+                peak = jnp.maximum(peak, fold(score, jnp.maximum))
+            inner_ref[:, at] = jnp.max(peak, axis=0, keepdims=True)
         for at in blocks:
-            weight = jnp.exp2((prob_ref[:, at] - inner_ref[:, at]) * factor)
-            prob_ref[:, at] = weight
-            inner_ref[:, at] = 1.0 / jnp.sum(weight, axis=0, keepdims=True)
+            total = jnp.zeros((PAD, step), jnp.float32)
+            for t in range(0, count, tile):
+                weight = jnp.exp2((prob_ref[t:t + tile, at] - inner_ref[:, at]) * factor)
+                prob_ref[t:t + tile, at] = weight
+                total = total + fold(weight, jnp.add)
+            inner_ref[:, at] = 1.0 / jnp.sum(total, axis=0, keepdims=True)
         for at in blocks:
             prob = prob_ref[:, at] * inner_ref[:, at]
             prob_ref[:, at] = prob
@@ -210,7 +224,7 @@
             short = diff.astype(jnp.bfloat16)
             diff_ref[at, :] = short.T
             inner_ref[:, at] = jnp.sum(short.astype(jnp.float32) * out, axis=0, keepdims=True) / mass
-        loss_ref[...] = jnp.full(loss_ref.shape, jnp.sum(squares), jnp.float32)
+        grad_ref[half:, :] = jnp.full((PAD, 2 * width), jnp.sum(squares), jnp.float32)
         gradient_half(
             pl.multiple_of((1 - core) * half, half),
             half, q_ref, prob_ref, cast_ref, diff_ref, inner_ref, values_ref, grad_ref, dscore_ref, scale,
@@ -219,13 +233,12 @@
     return call(
         kernel,
         [
-            ((half, 2 * width), jnp.float32),
+            ((half + PAD, 2 * width), jnp.float32),
             ((count, rows), jnp.float32),
             ((count, rows), jnp.bfloat16),
             ((rows, width), jnp.bfloat16),
             ((1, rows), jnp.float32),
             ((count, width), jnp.bfloat16),
-            ((PAD, LANES), jnp.float32),
         ],
         [queries, teach, *slots, *other],
         [pltpu.VMEM((count, width), jnp.bfloat16), pltpu.VMEM((half, rows), jnp.bfloat16)],
@@ -252,12 +265,12 @@
     )
 
 
-def packed(own, got, loss, heard, per):
+def packed(own, away, got, per):
     half, wide = own.shape
     blocks = half // per
 
-    def kernel(own_ref, got_ref, loss_ref, heard_ref, out_ref):
-        squares = loss_ref[...] + heard_ref[...]
+    def kernel(own_ref, away_ref, got_ref, out_ref):
+        squares = away_ref[half:, :LANES] + got_ref[half:, :LANES]
         one = squares.astype(jnp.bfloat16)
         left = squares - one.astype(jnp.float32)
         two = left.astype(jnp.bfloat16)
@@ -274,7 +287,7 @@
             for at in range(0, wide, LANES):
                 out_ref[b, per:, pl.ds(at, LANES)] = parts
 
-    return call(kernel, [((blocks, per + PAD, wide), jnp.bfloat16)], [own, got, loss, heard])[0]
+    return call(kernel, [((blocks, per + PAD, wide), jnp.bfloat16)], [own, away, got])[0]
 
 
 def update(heard, slot_params, first_moment, second_moment, terms):
@@ -348,7 +361,7 @@
 
     column = [copies]
     for d in range(1, n_qry):
-        column.append(lax.ppermute(copies, "qry", [(i, (i + d) % n_qry) for i in range(n_qry)]))
+        column.append(lax.ppermute(copies, "qry", [(peer(i, d, n_qry), i) for i in range(n_qry)]))
     slots = {0: jnp.concatenate(column, axis=0)}
     for j in chips:
         slots[j] = swap(slots[j ^ low[j]], low[j])
@@ -363,9 +376,9 @@
         state = teacher(live, flat, [(j, cache[j]) for j in offsets], state, last, scale)
     teacher_rows, teacher_turned = state
 
-    away, prob, cast, diff, inner, values, loss = student(flat, teacher_turned, slots, other, per, half, scale)
+    away, prob, cast, diff, inner, values = student(flat, teacher_turned, slots, other, per, half, scale)
     own, teacher_out = own_half(flat, teacher_rows, prob, cast, diff, inner, values, half, scale)
-    sent = packed(own, swap(away, 1), loss, swap(loss, 1), per)
+    sent = packed(own, away, swap(away, 1), per)
 
     groups = [[(2 * x + c) * n_qry + q for x in range(n_chip) for q in range(n_qry)] for c in range(2)]
     heard = lax.all_to_all(sent, ("keys", "qry"), 0, 0, axis_index_groups=groups, tiled=True)

time: 45.6 us -> 46 us (level)
  blocking collectives: 15.8 us -> 16.8 us
    all_to_all x1, blocking collectives: 15.8 us -> 16.8 us  [body(): lax.all_to_all(sent, ('keys', 'qry'), 0, 0, axis_index_groups=groups, til...]
    ppermute x3, waiting for transfers between devices: 2.56 us -> 1.88 us  [body(): lax.ppermute(copies, 'qry', [(peer(i, d, n_qry), i) for i in range(n_qry)])]
    ppermute x8 -> x7, waiting for transfers between devices: 3.77 us -> 4.41 us  [swap(): return lax.ppermute(block, 'keys', [(k, k ^ bit) for k in range(n_keys)])]
    ppermute x8 -> x7, starting transfers between devices: 4.28 us -> 4.34 us  [swap(): return lax.ppermute(block, 'keys', [(k, k ^ bit) for k in range(n_keys)])]
  transfers between devices with their start and end apart: 11 -> 10, of which waited for: 4 -> 5; matrix products, arithmetic and copies ran while one was open for 0% -> 0% of each run, Pallas kernels for 10% -> 10%
where the time goes in v2:
time: 46 us; the launch traced here: 45.8 us
  blocking collectives  16.8 us (37%)
  starting transfers between devices  10.1 us (22%)
  Pallas kernels  9.78 us (21%)
  waiting for transfers between devices  6.29 us (14%)
  between operations  2.7 us (6%)
    all_to_all x1, blocking collectives, body(): lax.all_to_all(sent, ('keys', 'qry'), 0, 0, axis_index_groups=groups, til...  16.8 us
    pallas_call x8, Pallas kernels, call(): pl.pallas_call(kernel, out_shape=tuple((space(s, d) for space, (s, d) in...  8.62 us
    ppermute x3, starting transfers between devices, body(): lax.ppermute(copies, 'qry', [(peer(i, d, n_qry), i) for i in range(n_qry)])  5.78 us
    ppermute x7, waiting for transfers between devices, swap(): return lax.ppermute(block, 'keys', [(k, k ^ bit) for k in range(n_keys)])  4.41 us
    ppermute x7, starting transfers between devices, swap(): return lax.ppermute(block, 'keys', [(k, k ^ bit) for k in range(n_keys)])  4.34 us
    ppermute x3, waiting for transfers between devices, body(): lax.ppermute(copies, 'qry', [(peer(i, d, n_qry), i) for i in range(n_qry)])  1.88 us
    pallas_call x1, Pallas kernels, load(): pl.pallas_call(kernel, out_shape=(pltpu.VMEM(slot_params.shape, jnp.bfloa...  1.15 us
  transfers between devices with their start and end apart: 10, of which 5 were waited for; matrix products, arithmetic and copies ran while one was open for 0% of the time, Pallas kernels for 10%

profile of v2, /device:TPU:0, one launch (start us, length us, event | category | flops | bytes accessed | tf_op | source)
XLA Modules:
  0.0 45.8 jit_solution(15240078240315911095)
XLA Ops:
  0.6 1.2 %load.1 = (bf16[64,256]{1,0:T(8,128)(2,1)S(1)}, bf16[1024,128]{1,0:T(8,128)(2,1)S(1)}, bf16[1024,128]{1,0:T(8,128)(2,1)S(1)}) custom-call(f32[64,256]{1,0:T(8,128)} %params_ref.1, bf16[512,128]{1,0:T(8,128)(2,1)} %refs_1_.1, bf16[512,128]{1,0:T(8,128)(2,1)} %refs_2_.1, bf16[1024,128]{1,0:T(8,128)(2,1)} %bitcast.10), custom_call_target="tpu_custom_call" | custom-call | tf_op jit(solution)/shard_map/load/pallas_call | solution.py:77
  1.8 5.1 %collective-permute-start.5 = (bf16[64,256]{1,0:T(8,128)(2,1)S(1)}, bf16[64,256]{1,0:T(8,128)(2,1)S(1)}, u32[]{:S(2)}, u32[]{:S(2)}) collective-permute-start(bf16[64,256]{1,0:T(8,128)(2,1)S(1)} %get-tuple-element.40), channel_id=1, source_target_pairs={{3,0},{2,1},{1,2},{0,3},{7,4},{6,5},{5,6},{4,7},{11,8},{10,9},{9,1... | collective-permute-start | bytes 98312 | tf_op jit(solution)/shard_map/ppermute | solution.py:364
  6.9 0.0 collective-permute-start.4
  6.9 0.6 %collective-permute-start.3 = (bf16[64,256]{1,0:T(8,128)(2,1)S(1)}, bf16[64,256]{1,0:T(8,128)(2,1)S(1)}, u32[]{:S(2)}, u32[]{:S(2)}) collective-permute-start(bf16[64,256]{1,0:T(8,128)(2,1)S(1)} %get-tuple-element.40), channel_id=1, source_target_pairs={{1,0},{0,1},{3,2},{2,3},{5,4},{4,5},{7,6},{6,7},{9,8},{8,9},{11,10... | collective-permute-start | bytes 98312 | tf_op jit(solution)/shard_map/ppermute | solution.py:364
  7.6 0.0 collective-permute-start.2
  7.6 1.6 %collective-permute-start = (bf16[1024,128]{1,0:T(8,128)(2,1)S(1)}, bf16[1024,128]{1,0:T(8,128)(2,1)S(1)}, u32[]{:S(2)}, u32[]{:S(2)}) collective-permute-start(bf16[1024,128]{1,0:T(8,128)(2,1)S(1)} %get-tuple-element.31.refs_0_), channel_id=1, source_target_pairs={{0,8},{4,12},{8,0},{12,4},{1,9},{5,13},{9,1},{13,5},{2,10},{6,14},... | collective-permute-start | bytes 786440 | tf_op jit(solution)/shard_map/ppermute | solution.py:346
  9.9 1.0 %collective-permute-done.3 = bf16[64,256]{1,0:T(8,128)(2,1)S(1)} collective-permute-done((bf16[64,256]{1,0:T(8,128)(2,1)S(1)}, bf16[64,256]{1,0:T(8,128)(2,1)S(1)}, u32[]{:S(2)}, u32[]{:S(2)}) %collective-permute-start.3) | collective-permute-done | bytes 32800 | tf_op jit(solution)/shard_map/ppermute | solution.py:364
  10.9 0.9 %collective-permute-done.4 = bf16[64,256]{1,0:T(8,128)(2,1)S(1)} collective-permute-done((bf16[64,256]{1,0:T(8,128)(2,1)S(1)}, bf16[64,256]{1,0:T(8,128)(2,1)S(1)}, u32[]{:S(2)}, u32[]{:S(2)}) %collective-permute-start.4) | collective-permute-done | bytes 32800 | tf_op jit(solution)/shard_map/ppermute | solution.py:364
  11.8 0.0 collective-permute-done.5
  11.8 1.6 %collective-permute-start.6 = (bf16[256,256]{1,0:T(8,128)(2,1)S(1)}, bf16[256,256]{1,0:T(8,128)(2,1)S(1)}, u32[]{:S(2)}, u32[]{:S(2)}) collective-permute-start(bf16[256,256]{1,0:T(8,128)(2,1)S(1)} %constant_dynamic-update-slice_fusion.refs_0_), channel_id=1, source_target_pairs={{0,8},{4,12},{8,0},{12,4},{1,9},{5,13},{9,1},{13,5},{2,10},{6,14},... | collective-permute-start | bytes 393224 | tf_op jit(solution)/shard_map/ppermute | solution.py:346
  14.0 2.8 %collective-permute-done.refs_0_ = bf16[1024,128]{1,0:T(8,128)(2,1)S(1)} collective-permute-done((bf16[1024,128]{1,0:T(8,128)(2,1)S(1)}, bf16[1024,128]{1,0:T(8,128)(2,1)S(1)}, u32[]{:S(2)}, u32[]{:S(2)}) %collective-permute-start) | collective-permute-done | bytes 262176 | tf_op jit(solution)/shard_map/ppermute | solution.py:346
  16.8 0.0 collective-permute-start.1
  17.4 0.6 %collective-permute-start.7 = (bf16[256,256]{1,0:T(8,128)(2,1)S(1)}, bf16[256,256]{1,0:T(8,128)(2,1)S(1)}, u32[]{:S(2)}, u32[]{:S(2)}) collective-permute-start(bf16[256,256]{1,0:T(8,128)(2,1)S(1)} %constant_dynamic-update-slice_fusion.refs_0_), channel_id=1, source_target_pairs={{0,4},{4,0},{8,12},{12,8},{1,5},{5,1},{9,13},{13,9},{2,6},{6,2},{1... | collective-permute-start | bytes 393224 | tf_op jit(solution)/shard_map/ppermute | solution.py:346
  18.0 1.1 %collective-permute-done.6.refs_1_ = bf16[256,256]{1,0:T(8,128)(2,1)S(1)} collective-permute-done((bf16[256,256]{1,0:T(8,128)(2,1)S(1)}, bf16[256,256]{1,0:T(8,128)(2,1)S(1)}, u32[]{:S(2)}, u32[]{:S(2)}) %collective-permute-start.6) | collective-permute-done | bytes 131104 | tf_op jit(solution)/shard_map/ppermute | solution.py:346
  19.1 0.0 collective-permute-start.8
  19.1 0.1 fusion.1.live_ref
  19.2 1.1 %shard_map.136 = (f32[1,1024]{1,0:T(1,128)S(1)}, f32[136,1024]{1,0:T(8,128)S(1)}) custom-call(s32[8,128]{1,0:T(8,128)S(1)} %fusion.1.live_ref, bf16[1024,128]{1,0:T(8,128)(2,1)S(1)} %get-tuple-element.30.q_ref, bf16[1024,128]{1,0:T(8,128)(2,1)S(1)} %get-tuple-element.31.refs_0_), custom_call_target="tpu_custom_call" | custom-call | tf_op jit(solution)/shard_map/pallas_call | solution.py:52
  20.3 0.0 collective-permute-done.2.refs_0_
  20.3 1.1 %shard_map.137 = (f32[1,1024]{1,0:T(1,128)S(1)}, f32[136,1024]{1,0:T(8,128)S(1)}) custom-call(s32[8,128]{1,0:T(8,128)S(1)} %fusion.1.live_ref, bf16[1024,128]{1,0:T(8,128)(2,1)S(1)} %get-tuple-element.30.q_ref, bf16[1024,128]{1,0:T(8,128)(2,1)S(1)} %collective-permute-done.2.refs_0_, f32[1,1024]{1,0:T(1,128)S(1)} %get-tuple-element.32.refs_1_, ...), custom_call_target="tpu_custom_call" | custom-call | tf_op jit(solution)/shard_map/pallas_call | solution.py:52
  21.5 1.1 %shard_map.138 = (f32[1,1024]{1,0:T(1,128)S(1)}, f32[136,1024]{1,0:T(8,128)S(1)}) custom-call(s32[8,128]{1,0:T(8,128)S(1)} %fusion.1.live_ref, bf16[1024,128]{1,0:T(8,128)(2,1)S(1)} %get-tuple-element.30.q_ref, bf16[1024,128]{1,0:T(8,128)(2,1)S(1)} %collective-permute-done.refs_0_, f32[1,1024]{1,0:T(1,128)S(1)} %get-tuple-element.34.refs_1_, ...), custom_call_target="tpu_custom_call" | custom-call | tf_op jit(solution)/shard_map/pallas_call | solution.py:52
  22.6 0.0 collective-permute-done.1.refs_0_
  22.6 0.3 shard_map.139
  23.0 0.0 collective-permute-done.7.refs_2_
  23.0 0.0 collective-permute-done.8.refs_3_
  23.0 3.0 %shard_map.140 = (f32[520,256]{1,0:T(8,128)S(1)}, f32[1024,1024]{1,0:T(8,128)S(1)}, bf16[1024,1024]{1,0:T(8,128)(2,1)S(1)}, bf16[1024,128]{1,0:T(8,128)(2,1)S(1)...) custom-call(bf16[1024,128]{1,0:T(8,128)(2,1)S(1)} %get-tuple-element.30.q_ref, ...), custom_call_target="tpu_custom_call" | custom-call | tf_op jit(solution)/shard_map/pallas_call | solution.py:52
  26.0 0.6 %collective-permute-start.9 = (f32[520,256]{1,0:T(8,128)S(1)}, f32[520,256]{1,0:T(8,128)S(1)}, u32[]{:S(2)}, u32[]{:S(2)}) collective-permute-start(f32[520,256]{1,0:T(8,128)S(1)} %get-tuple-element.48.away_ref), channel_id=1, source_target_pairs={{0,4},{4,0},{8,12},{12,8},{1,5},{5,1},{9,13},{13,9},{2,6},{6,2},{1... | collective-permute-start | bytes 1597448 | tf_op jit(solution)/shard_map/ppermute | solution.py:346
  26.6 0.0 copy-start
  26.6 0.0 copy-start.1
  26.6 0.0 copy-start.2
  26.6 1.0 %shard_map.141 = (f32[512,256]{1,0:T(8,128)S(1)}, bf16[1024,128]{1,0:T(8,128)(2,1)}) custom-call(bf16[1024,128]{1,0:T(8,128)(2,1)S(1)} %get-tuple-element.38.rows_ref, bf16[1024,128]{1,0:T(8,128)(2,1)S(1)} %get-tuple-element.30.q_ref, f32[1024,1024]{1,0:T(8,128)S(1)} %get-tuple-element.41.prob_ref, bf16[1024,1024]{1,0:T(8,128)(2,1)S(1)} %get-tuple-element.42.cast_ref, ...), custom_call_target="tpu_custom_call" | custom-call | tf_op jit(solution)/shard_map/pallas_call | solution.py:52
  27.6 0.5 %collective-permute-done.9.got_ref = f32[520,256]{1,0:T(8,128)S(1)} collective-permute-done((f32[520,256]{1,0:T(8,128)S(1)}, f32[520,256]{1,0:T(8,128)S(1)}, u32[]{:S(2)}, u32[]{:S(2)}) %collective-permute-start.9) | collective-permute-done | bytes 532512 | tf_op jit(solution)/shard_map/ppermute | solution.py:346
  28.2 0.1 shard_map.142
  28.2 16.8 %all_to_all.5.heard_ref = bf16[8,72,256]{2,1,0:T(8,128)(2,1)S(1)} all-to-all(bf16[8,72,256]{2,1,0:T(8,128)(2,1)S(1)} %shard_map.142), channel_id=1, replica_groups={{0,1,2,3,8,9,10,11},{4,5,6,7,12,13,14,15},{16,17,18,19,24,25,26,27},{20..., dimensions={0} | all-to-all | bytes 589824 | tf_op jit(solution)/shard_map/all_to_all | solution.py:384
  45.0 0.0 copy-done
  45.0 0.0 copy-done.1
  45.0 0.0 copy-done.2
  45.0 0.8 %shard_map.143 = (f32[64,256]{1,0:T(8,128)}, f32[64,256]{1,0:T(8,128)}, f32[64,256]{1,0:T(8,128)}, f32[64,256]{1,0:T(8,128)}, f32[1,128]{1,0:T(1,128)}) custom-call(bf16[8,72,256]{2,1,0:T(8,128)(2,1)S(1)} %all_to_all.5.heard_ref, f32[64,256]{1,0:T(8,128)S(1)} %copy-done, f32[64,256]{1,0:T(8,128)S(1)} %copy-done.1, f32[64,256]{1,0:T(8,128)S(1)} %copy-done.2), custom_call_target="tpu_custom_call" | custom-call | tf_op jit(solution)/shard_map/pallas_call | solution.py:52
  (7 shorter events, 0.0 us)
Async XLA Ops:
  1.8 10.0 %collective-permute-start.5 = (bf16[64,256]{1,0:T(8,128)(2,1)S(1)}, bf16[64,256]{1,0:T(8,128)(2,1)S(1)}, u32[]{:S(2)}, u32[]{:S(2)}) collective-permute-start(bf16[64,256]{1,0:T(8,128)(2,1)S(1)} %get-tuple-element.40), channel_id=1, source_target_pairs={{3,0},{2,1},{1,2},{0,3},{7,4},{6,5},{5,6},{4,7},{11,8},{10,9},{9,1... | collective-permute-start | bytes 98312 | tf_op jit(solution)/shard_map/ppermute | solution.py:364
  6.9 4.8 %collective-permute-start.4 = (bf16[64,256]{1,0:T(8,128)(2,1)S(1)}, bf16[64,256]{1,0:T(8,128)(2,1)S(1)}, u32[]{:S(2)}, u32[]{:S(2)}) collective-permute-start(bf16[64,256]{1,0:T(8,128)(2,1)S(1)} %get-tuple-element.40), channel_id=1, source_target_pairs={{2,0},{3,1},{0,2},{1,3},{6,4},{7,5},{4,6},{5,7},{10,8},{11,9},{8,1... | collective-permute-start | bytes 98312 | tf_op jit(solution)/shard_map/ppermute | solution.py:364
  6.9 3.9 %collective-permute-start.3 = (bf16[64,256]{1,0:T(8,128)(2,1)S(1)}, bf16[64,256]{1,0:T(8,128)(2,1)S(1)}, u32[]{:S(2)}, u32[]{:S(2)}) collective-permute-start(bf16[64,256]{1,0:T(8,128)(2,1)S(1)} %get-tuple-element.40), channel_id=1, source_target_pairs={{1,0},{0,1},{3,2},{2,3},{5,4},{4,5},{7,6},{6,7},{9,8},{8,9},{11,10... | collective-permute-start | bytes 98312 | tf_op jit(solution)/shard_map/ppermute | solution.py:364
  7.6 12.8 %collective-permute-start.2 = (bf16[1024,128]{1,0:T(8,128)(2,1)S(1)}, bf16[1024,128]{1,0:T(8,128)(2,1)S(1)}, u32[]{:S(2)}, u32[]{:S(2)}) collective-permute-start(bf16[1024,128]{1,0:T(8,128)(2,1)S(1)} %get-tuple-element.31.refs_0_), channel_id=1, source_target_pairs={{0,4},{4,0},{8,12},{12,8},{1,5},{5,1},{9,13},{13,9},{2,6},{6,2},{1... | collective-permute-start | bytes 786440 | tf_op jit(solution)/shard_map/ppermute | solution.py:346
  7.6 9.2 %collective-permute-start = (bf16[1024,128]{1,0:T(8,128)(2,1)S(1)}, bf16[1024,128]{1,0:T(8,128)(2,1)S(1)}, u32[]{:S(2)}, u32[]{:S(2)}) collective-permute-start(bf16[1024,128]{1,0:T(8,128)(2,1)S(1)} %get-tuple-element.31.refs_0_), channel_id=1, source_target_pairs={{0,8},{4,12},{8,0},{12,4},{1,9},{5,13},{9,1},{13,5},{2,10},{6,14},... | collective-permute-start | bytes 786440 | tf_op jit(solution)/shard_map/ppermute | solution.py:346
  11.8 7.3 %collective-permute-start.6 = (bf16[256,256]{1,0:T(8,128)(2,1)S(1)}, bf16[256,256]{1,0:T(8,128)(2,1)S(1)}, u32[]{:S(2)}, u32[]{:S(2)}) collective-permute-start(bf16[256,256]{1,0:T(8,128)(2,1)S(1)} %constant_dynamic-update-slice_fusion.refs_0_), channel_id=1, source_target_pairs={{0,8},{4,12},{8,0},{12,4},{1,9},{5,13},{9,1},{13,5},{2,10},{6,14},... | collective-permute-start | bytes 393224 | tf_op jit(solution)/shard_map/ppermute | solution.py:346
  16.8 5.9 %collective-permute-start.1 = (bf16[1024,128]{1,0:T(8,128)(2,1)S(1)}, bf16[1024,128]{1,0:T(8,128)(2,1)S(1)}, u32[]{:S(2)}, u32[]{:S(2)}) collective-permute-start(bf16[1024,128]{1,0:T(8,128)(2,1)S(1)} %collective-permute-done.refs_0_), channel_id=1, source_target_pairs={{0,4},{4,0},{8,12},{12,8},{1,5},{5,1},{9,13},{13,9},{2,6},{6,2},{1... | collective-permute-start | bytes 786440 | tf_op jit(solution)/shard_map/ppermute | solution.py:346
  17.4 5.5 %collective-permute-start.7 = (bf16[256,256]{1,0:T(8,128)(2,1)S(1)}, bf16[256,256]{1,0:T(8,128)(2,1)S(1)}, u32[]{:S(2)}, u32[]{:S(2)}) collective-permute-start(bf16[256,256]{1,0:T(8,128)(2,1)S(1)} %constant_dynamic-update-slice_fusion.refs_0_), channel_id=1, source_target_pairs={{0,4},{4,0},{8,12},{12,8},{1,5},{5,1},{9,13},{13,9},{2,6},{6,2},{1... | collective-permute-start | bytes 393224 | tf_op jit(solution)/shard_map/ppermute | solution.py:346
  19.1 3.9 %collective-permute-start.8 = (bf16[256,256]{1,0:T(8,128)(2,1)S(1)}, bf16[256,256]{1,0:T(8,128)(2,1)S(1)}, u32[]{:S(2)}, u32[]{:S(2)}) collective-permute-start(bf16[256,256]{1,0:T(8,128)(2,1)S(1)} %collective-permute-done.6.refs_1_), channel_id=1, source_target_pairs={{0,4},{4,0},{8,12},{12,8},{1,5},{5,1},{9,13},{13,9},{2,6},{6,2},{1... | collective-permute-start | bytes 393224 | tf_op jit(solution)/shard_map/ppermute | solution.py:346
  26.0 2.1 %collective-permute-start.9 = (f32[520,256]{1,0:T(8,128)S(1)}, f32[520,256]{1,0:T(8,128)S(1)}, u32[]{:S(2)}, u32[]{:S(2)}) collective-permute-start(f32[520,256]{1,0:T(8,128)S(1)} %get-tuple-element.48.away_ref), channel_id=1, source_target_pairs={{0,4},{4,0},{8,12},{12,8},{1,5},{5,1},{9,13},{13,9},{2,6},{6,2},{1... | collective-permute-start | bytes 1597448 | tf_op jit(solution)/shard_map/ppermute | solution.py:346
  26.6 18.4 %copy-start = (f32[64,256]{1,0:T(8,128)S(1)}, f32[64,256]{1,0:T(8,128)}, u32[]{:S(2)}) copy-start(f32[64,256]{1,0:T(8,128)} %params_ref.1) | copy-start | bytes 196612
  26.6 18.4 %copy-start.1 = (f32[64,256]{1,0:T(8,128)S(1)}, f32[64,256]{1,0:T(8,128)}, u32[]{:S(2)}) copy-start(f32[64,256]{1,0:T(8,128)} %first_ref.1) | copy-start | bytes 196612
  26.6 18.4 %copy-start.2 = (f32[64,256]{1,0:T(8,128)S(1)}, f32[64,256]{1,0:T(8,128)}, u32[]{:S(2)}) copy-start(f32[64,256]{1,0:T(8,128)} %second_ref.1) | copy-start | bytes 196612

commit v3 on v2

--- a/solution.py
+++ b/solution.py
@@ -63,6 +63,8 @@
     size, width = keys.shape
     ins = [pltpu.with_memory_space_constraint(a, pltpu.HBM) for a in (slot_params, keys, values, queries)]
 
+    per = slot_params.shape[0]
+
     def kernel(*refs):
         sources, (slots_ref, cache_ref, q_ref, full_ref, sems) = refs[:4], refs[4:]
         targets = (full_ref, cache_ref.at[pl.ds(0, size)], cache_ref.at[pl.ds(size, size)], q_ref)
@@ -70,7 +72,10 @@
         for move in moves:
             move.start()
         moves[0].wait()
-        slots_ref[...] = full_ref[...].astype(jnp.bfloat16)
+        slots = full_ref[...].astype(jnp.bfloat16)
+        slots_ref[...] = slots
+        cache_ref[2 * size:2 * size + per, :] = slots[:, :width]
+        cache_ref[2 * size + per:, :] = slots[:, width:]
         for move in moves[1:]:
             move.wait()
 
@@ -78,7 +83,7 @@
         kernel,
         out_shape=(
             pltpu.VMEM(slot_params.shape, jnp.bfloat16),
-            pltpu.VMEM((2 * size, width), keys.dtype),
+            pltpu.VMEM((2 * (size + per), width), keys.dtype),
             pltpu.VMEM(queries.shape, queries.dtype),
         ),
         in_specs=[pl.BlockSpec(memory_space=pltpu.HBM)] * 4,
@@ -92,7 +97,7 @@
     )(*ins)
 
 
-def teacher(live, queries, segments, state, last, scale):
+def teacher(live, queries, segments, size, state, last, scale):
     rows, width = queries.shape
     step = row_block(rows)
     shapes = [((1, rows), jnp.float32), ((width + PAD, rows), jnp.float32)]
@@ -117,7 +122,6 @@
         blocks = [pl.ds(at, step) for at in range(0, rows, step)]
         for s, offset in enumerate(offsets):
             cache_ref = seg[s]
-            size = cache_ref.shape[0] // 2
             tile = math.gcd(size, TILE)
             count = jnp.max(live_ref[offset:offset + 1, :])
 
@@ -125,7 +129,7 @@
             def _():
                 live = lax.broadcasted_iota(jnp.int32, (size, width), 0) < count
                 keys = jnp.where(live, cache_ref[:size, :], cache_ref[:1, :])
-                turned = with_ones(cache_ref[size:, :])
+                turned = with_ones(cache_ref[size:2 * size, :])
                 turned = jnp.where(
                     lax.broadcasted_iota(jnp.int32, turned.shape, 1) < count, turned, jnp.zeros_like(turned)
                 )
@@ -155,7 +159,7 @@
     arrays = [queries] + [a for _, a in segments] + ([] if first else list(state))
     scratch = [pltpu.VMEM(s, d) for s, d in shapes] if last else []
     scratch += [
-        pltpu.VMEM((segments[0][1].shape[0] // 2, rows), jnp.float32), pltpu.VMEM((1, rows), jnp.float32)
+        pltpu.VMEM((size, rows), jnp.float32), pltpu.VMEM((1, rows), jnp.float32)
     ]
     return call(kernel, ends if last else shapes, [live] + arrays, scratch)
 
@@ -172,29 +176,37 @@
     grad_ref[:half, :width] = nn(dscore_ref[...], q_ref[...]) * scale
 
 
-def student(queries, teach, slots, other, per, half, scale):
+def student(queries, teach, caches, slots, other, per, half, scale):
     rounds = len(slots)
+    n_caches = len(caches)
     rows, width = queries.shape
     step = row_block(rows)
     pieces = slots[0].shape[0] // per
-    count = 2 * rounds * pieces * per
+    count = 2 * rounds * (pieces + 1) * per
+    tail = caches[0].shape[0] - 2 * per
     tile = math.gcd(count, TILE)
     factor = scale * math.log2(math.e)
 
     def kernel(q_ref, teach_ref, *refs):
+        near, refs = refs[:n_caches], refs[n_caches:]
         sources, refs = refs[: 2 * rounds], refs[2 * rounds:]
         grad_ref, prob_ref, cast_ref, diff_ref, inner_ref, values_ref, keys_ref, dscore_ref = refs
         n_chip, n_qry = lax.axis_size("keys") // 2, lax.axis_size("qry")
         me, mine = lax.axis_index("keys"), lax.axis_index("qry")
         core, chip = lax.rem(me, 2), lax.div(me, 2)
+
+        def put(c, x, index, keys, values):
+            to = pl.multiple_of(((c * n_chip + (chip ^ x)) * n_qry + index) * per, per)
+            keys_ref[pl.ds(to, per), :] = keys
+            values_ref[pl.ds(to, per), :] = values
+
+        for j, source in enumerate(near):
+            put(core ^ (j & 1), j // 2, mine, source[tail:tail + per, :], source[tail + per:, :])
         for r, source in enumerate(sources):
             c, x = (core, r) if r < rounds else (1 - core, r - rounds)
             for d in range(pieces):
-                place = (c * n_chip + (chip ^ x)) * n_qry + peer(mine, d, n_qry)
-                to = pl.multiple_of(place * per, per)
                 piece = source[pl.ds(d * per, per), :]
-                keys_ref[pl.ds(to, per), :] = piece[:, :width]
-                values_ref[pl.ds(to, per), :] = piece[:, width:]
+                put(c, x, peer(mine, d + 1, n_qry), piece[:, :width], piece[:, width:])
         turned = with_ones(values_ref[...])
         squares = jnp.zeros((width, step), jnp.float32)
         blocks = [pl.ds(at, step) for at in range(0, rows, step)]
@@ -240,7 +252,7 @@
             ((1, rows), jnp.float32),
             ((count, width), jnp.bfloat16),
         ],
-        [queries, teach, *slots, *other],
+        [queries, teach, *caches, *slots, *other],
         [pltpu.VMEM((count, width), jnp.bfloat16), pltpu.VMEM((half, rows), jnp.bfloat16)],
     )
 
@@ -359,7 +371,7 @@
     for j in list(chips) + list(range(1, n_keys, 2)):
         cache[j] = swap(cache[j ^ low[j]], low[j])
 
-    column = [copies]
+    column = []
     for d in range(1, n_qry):
         column.append(lax.ppermute(copies, "qry", [(peer(i, d, n_qry), i) for i in range(n_qry)]))
     slots = {0: jnp.concatenate(column, axis=0)}
@@ -373,10 +385,12 @@
     state = None
     for name, offsets in stages:
         last = name == stages[-1][0]
-        state = teacher(live, flat, [(j, cache[j]) for j in offsets], state, last, scale)
+        state = teacher(live, flat, [(j, cache[j]) for j in offsets], cache_keys.shape[0], state, last, scale)
     teacher_rows, teacher_turned = state
 
-    away, prob, cast, diff, inner, values = student(flat, teacher_turned, slots, other, per, half, scale)
+    away, prob, cast, diff, inner, values = student(
+        flat, teacher_turned, [cache[j] for j in range(n_keys)], slots, other, per, half, scale
+    )
     own, teacher_out = own_half(flat, teacher_rows, prob, cast, diff, inner, values, half, scale)
     sent = packed(own, away, swap(away, 1), per)
 

time: 46 us -> 45.9 us (level)
    ppermute x7, waiting for transfers between devices: 4.41 us -> 5.8 us  [swap(): return lax.ppermute(block, 'keys', [(k, k ^ bit) for k in range(n_keys)])]
    ppermute x3, waiting for transfers between devices: 1.88 us -> 0.54 us  [body(): lax.ppermute(copies, 'qry', [(peer(i, d, n_qry), i) for i in range(n_qry)])]
  transfers between devices with their start and end apart: 10 -> 10, of which waited for: 5 -> 4; matrix products, arithmetic and copies ran while one was open for 0% -> 0% of each run, Pallas kernels for 10% -> 10%
where the time goes in v3:
time: 45.9 us; the launch traced here: 45.7 us
  blocking collectives  16.8 us (37%)
  starting transfers between devices  10.1 us (22%)
  Pallas kernels  9.71 us (21%)
  waiting for transfers between devices  6.35 us (14%)
  between operations  2.71 us (6%)
    all_to_all x1, blocking collectives, body(): lax.all_to_all(sent, ('keys', 'qry'), 0, 0, axis_index_groups=groups, til...  16.8 us
    pallas_call x8, Pallas kernels, call(): pl.pallas_call(kernel, out_shape=tuple((space(s, d) for space, (s, d) in...  8.56 us
    ppermute x7, waiting for transfers between devices, swap(): return lax.ppermute(block, 'keys', [(k, k ^ bit) for k in range(n_keys)])  5.8 us
    ppermute x3, starting transfers between devices, body(): lax.ppermute(copies, 'qry', [(peer(i, d, n_qry), i) for i in range(n_qry)])  5.78 us
    ppermute x7, starting transfers between devices, swap(): return lax.ppermute(block, 'keys', [(k, k ^ bit) for k in range(n_keys)])  4.29 us
    pallas_call x1, Pallas kernels, load(): pl.pallas_call(kernel, out_shape=(pltpu.VMEM(slot_params.shape, jnp.bfloa...  1.15 us
  transfers between devices with their start and end apart: 10, of which 4 were waited for; matrix products, arithmetic and copies ran while one was open for 0% of the time, Pallas kernels for 10%

profile of v3, /device:TPU:0, one launch (start us, length us, event | category | flops | bytes accessed | tf_op | source)
XLA Modules:
  0.0 45.7 jit_solution(6773232828126728438)
XLA Ops:
  0.6 1.2 %load.1 = (bf16[64,256]{1,0:T(8,128)(2,1)S(1)}, bf16[1152,128]{1,0:T(8,128)(2,1)S(1)}, bf16[1024,128]{1,0:T(8,128)(2,1)S(1)}) custom-call(f32[64,256]{1,0:T(8,128)} %params_ref.1, bf16[512,128]{1,0:T(8,128)(2,1)} %refs_1_.1, bf16[512,128]{1,0:T(8,128)(2,1)} %refs_2_.1, bf16[1024,128]{1,0:T(8,128)(2,1)} %bitcast.10), custom_call_target="tpu_custom_call" | custom-call | tf_op jit(solution)/shard_map/load/pallas_call | solution.py:82
  1.8 5.1 %collective-permute-start.5 = (bf16[64,256]{1,0:T(8,128)(2,1)S(1)}, bf16[64,256]{1,0:T(8,128)(2,1)S(1)}, u32[]{:S(2)}, u32[]{:S(2)}) collective-permute-start(bf16[64,256]{1,0:T(8,128)(2,1)S(1)} %get-tuple-element.40), channel_id=1, source_target_pairs={{3,0},{2,1},{1,2},{0,3},{7,4},{6,5},{5,6},{4,7},{11,8},{10,9},{9,1... | collective-permute-start | bytes 98312 | tf_op jit(solution)/shard_map/ppermute | solution.py:376
  6.9 0.0 collective-permute-start.4
  6.9 0.6 %collective-permute-start.3 = (bf16[64,256]{1,0:T(8,128)(2,1)S(1)}, bf16[64,256]{1,0:T(8,128)(2,1)S(1)}, u32[]{:S(2)}, u32[]{:S(2)}) collective-permute-start(bf16[64,256]{1,0:T(8,128)(2,1)S(1)} %get-tuple-element.40), channel_id=1, source_target_pairs={{1,0},{0,1},{3,2},{2,3},{5,4},{4,5},{7,6},{6,7},{9,8},{8,9},{11,10... | collective-permute-start | bytes 98312 | tf_op jit(solution)/shard_map/ppermute | solution.py:376
  7.6 0.0 collective-permute-start.2
  7.6 1.6 %collective-permute-start = (bf16[1152,128]{1,0:T(8,128)(2,1)S(1)}, bf16[1152,128]{1,0:T(8,128)(2,1)S(1)}, u32[]{:S(2)}, u32[]{:S(2)}) collective-permute-start(bf16[1152,128]{1,0:T(8,128)(2,1)S(1)} %get-tuple-element.31.refs_0_), channel_id=1, source_target_pairs={{0,8},{4,12},{8,0},{12,4},{1,9},{5,13},{9,1},{13,5},{2,10},{6,14},... | collective-permute-start | bytes 884744 | tf_op jit(solution)/shard_map/ppermute | solution.py:358
  11.2 0.0 collective-permute-done.3
  11.2 0.5 %collective-permute-done.4 = bf16[64,256]{1,0:T(8,128)(2,1)S(1)} collective-permute-done((bf16[64,256]{1,0:T(8,128)(2,1)S(1)}, bf16[64,256]{1,0:T(8,128)(2,1)S(1)}, u32[]{:S(2)}, u32[]{:S(2)}) %collective-permute-start.4) | collective-permute-done | bytes 32800 | tf_op jit(solution)/shard_map/ppermute | solution.py:376
  11.8 0.0 collective-permute-done.5
  11.8 1.6 %collective-permute-start.6 = (bf16[192,256]{1,0:T(8,128)(2,1)S(1)}, bf16[192,256]{1,0:T(8,128)(2,1)S(1)}, u32[]{:S(2)}, u32[]{:S(2)}) collective-permute-start(bf16[192,256]{1,0:T(8,128)(2,1)S(1)} %constant_dynamic-update-slice_fusion.refs_4_), channel_id=1, source_target_pairs={{0,8},{4,12},{8,0},{12,4},{1,9},{5,13},{9,1},{13,5},{2,10},{6,14},... | collective-permute-start | bytes 294920 | tf_op jit(solution)/shard_map/ppermute | solution.py:358
  13.3 4.1 %collective-permute-done.refs_0_.refs_2_ = bf16[1152,128]{1,0:T(8,128)(2,1)S(1)} collective-permute-done((bf16[1152,128]{1,0:T(8,128)(2,1)S(1)}, bf16[1152,128]{1,0:T(8,128)(2,1)S(1)}, u32[]{:S(2)}, u32[]{:S(2)}) %collective-permute-start) | collective-permute-done | bytes 294944 | tf_op jit(solution)/shard_map/ppermute | solution.py:358
  17.5 0.0 collective-permute-start.1
  17.5 0.5 %collective-permute-start.7 = (bf16[192,256]{1,0:T(8,128)(2,1)S(1)}, bf16[192,256]{1,0:T(8,128)(2,1)S(1)}, u32[]{:S(2)}, u32[]{:S(2)}) collective-permute-start(bf16[192,256]{1,0:T(8,128)(2,1)S(1)} %constant_dynamic-update-slice_fusion.refs_4_), channel_id=1, source_target_pairs={{0,4},{4,0},{8,12},{12,8},{1,5},{5,1},{9,13},{13,9},{2,6},{6,2},{1... | collective-permute-start | bytes 294920 | tf_op jit(solution)/shard_map/ppermute | solution.py:358
  18.0 1.1 %collective-permute-done.6.refs_5_ = bf16[192,256]{1,0:T(8,128)(2,1)S(1)} collective-permute-done((bf16[192,256]{1,0:T(8,128)(2,1)S(1)}, bf16[192,256]{1,0:T(8,128)(2,1)S(1)}, u32[]{:S(2)}, u32[]{:S(2)}) %collective-permute-start.6) | collective-permute-done | bytes 98336 | tf_op jit(solution)/shard_map/ppermute | solution.py:358
  19.1 0.0 collective-permute-start.8
  19.1 0.1 fusion.1.live_ref
  19.2 1.1 %shard_map.136 = (f32[1,1024]{1,0:T(1,128)S(1)}, f32[136,1024]{1,0:T(8,128)S(1)}) custom-call(s32[8,128]{1,0:T(8,128)S(1)} %fusion.1.live_ref, bf16[1024,128]{1,0:T(8,128)(2,1)S(1)} %get-tuple-element.30.q_ref, bf16[1152,128]{1,0:T(8,128)(2,1)S(1)} %get-tuple-element.31.refs_0_), custom_call_target="tpu_custom_call" | custom-call | tf_op jit(solution)/shard_map/pallas_call | solution.py:52
  20.3 0.0 collective-permute-done.2.refs_0_.refs_1_
  20.3 1.1 %shard_map.137 = (f32[1,1024]{1,0:T(1,128)S(1)}, f32[136,1024]{1,0:T(8,128)S(1)}) custom-call(s32[8,128]{1,0:T(8,128)S(1)} %fusion.1.live_ref, bf16[1024,128]{1,0:T(8,128)(2,1)S(1)} %get-tuple-element.30.q_ref, bf16[1152,128]{1,0:T(8,128)(2,1)S(1)} %collective-permute-done.2.refs_0_.refs_1_, f32[1,1024]{1,0:T(1,128)S(1)} %get-tuple-element.32.refs_1_, ...), custom_call_target="tpu_custom_call" | custom-call | tf_op jit(solution)/shard_map/pallas_call | solution.py:52
  21.5 1.1 %shard_map.138 = (f32[1,1024]{1,0:T(1,128)S(1)}, f32[136,1024]{1,0:T(8,128)S(1)}) custom-call(s32[8,128]{1,0:T(8,128)S(1)} %fusion.1.live_ref, bf16[1024,128]{1,0:T(8,128)(2,1)S(1)} %get-tuple-element.30.q_ref, bf16[1152,128]{1,0:T(8,128)(2,1)S(1)} %collective-permute-done.refs_0_.refs_2_, f32[1,1024]{1,0:T(1,128)S(1)} %get-tuple-element.34.refs_1_, ...), custom_call_target="tpu_custom_call" | custom-call | tf_op jit(solution)/shard_map/pallas_call | solution.py:52
  22.6 0.0 collective-permute-done.1.refs_0_.refs_3_
  22.6 0.3 shard_map.139
  23.0 0.0 collective-permute-done.7.refs_6_
  23.0 0.0 collective-permute-done.8.refs_7_
  23.0 3.0 %shard_map.140 = (f32[520,256]{1,0:T(8,128)S(1)}, f32[1024,1024]{1,0:T(8,128)S(1)}, bf16[1024,1024]{1,0:T(8,128)(2,1)S(1)}, bf16[1024,128]{1,0:T(8,128)(2,1)S(1)...) custom-call(bf16[1024,128]{1,0:T(8,128)(2,1)S(1)} %get-tuple-element.30.q_ref, ...), custom_call_target="tpu_custom_call" | custom-call | tf_op jit(solution)/shard_map/pallas_call | solution.py:52
  26.0 0.6 %collective-permute-start.9 = (f32[520,256]{1,0:T(8,128)S(1)}, f32[520,256]{1,0:T(8,128)S(1)}, u32[]{:S(2)}, u32[]{:S(2)}) collective-permute-start(f32[520,256]{1,0:T(8,128)S(1)} %get-tuple-element.48.away_ref), channel_id=1, source_target_pairs={{0,4},{4,0},{8,12},{12,8},{1,5},{5,1},{9,13},{13,9},{2,6},{6,2},{1... | collective-permute-start | bytes 1597448 | tf_op jit(solution)/shard_map/ppermute | solution.py:358
  26.6 0.0 copy-start
  26.6 0.0 copy-start.1
  26.6 0.0 copy-start.2
  26.6 1.0 %shard_map.141 = (f32[512,256]{1,0:T(8,128)S(1)}, bf16[1024,128]{1,0:T(8,128)(2,1)}) custom-call(bf16[1024,128]{1,0:T(8,128)(2,1)S(1)} %get-tuple-element.38.rows_ref, bf16[1024,128]{1,0:T(8,128)(2,1)S(1)} %get-tuple-element.30.q_ref, f32[1024,1024]{1,0:T(8,128)S(1)} %get-tuple-element.41.prob_ref, bf16[1024,1024]{1,0:T(8,128)(2,1)S(1)} %get-tuple-element.42.cast_ref, ...), custom_call_target="tpu_custom_call" | custom-call | tf_op jit(solution)/shard_map/pallas_call | solution.py:52
  27.6 0.5 %collective-permute-done.9.got_ref = f32[520,256]{1,0:T(8,128)S(1)} collective-permute-done((f32[520,256]{1,0:T(8,128)S(1)}, f32[520,256]{1,0:T(8,128)S(1)}, u32[]{:S(2)}, u32[]{:S(2)}) %collective-permute-start.9) | collective-permute-done | bytes 532512 | tf_op jit(solution)/shard_map/ppermute | solution.py:358
  28.1 0.1 shard_map.142
  28.2 16.8 %all_to_all.5.heard_ref = bf16[8,72,256]{2,1,0:T(8,128)(2,1)S(1)} all-to-all(bf16[8,72,256]{2,1,0:T(8,128)(2,1)S(1)} %shard_map.142), channel_id=1, replica_groups={{0,1,2,3,8,9,10,11},{4,5,6,7,12,13,14,15},{16,17,18,19,24,25,26,27},{20..., dimensions={0} | all-to-all | bytes 589824 | tf_op jit(solution)/shard_map/all_to_all | solution.py:398
  44.9 0.0 copy-done
  44.9 0.0 copy-done.1
  44.9 0.0 copy-done.2
  44.9 0.8 %shard_map.143 = (f32[64,256]{1,0:T(8,128)}, f32[64,256]{1,0:T(8,128)}, f32[64,256]{1,0:T(8,128)}, f32[64,256]{1,0:T(8,128)}, f32[1,128]{1,0:T(1,128)}) custom-call(bf16[8,72,256]{2,1,0:T(8,128)(2,1)S(1)} %all_to_all.5.heard_ref, f32[64,256]{1,0:T(8,128)S(1)} %copy-done, f32[64,256]{1,0:T(8,128)S(1)} %copy-done.1, f32[64,256]{1,0:T(8,128)S(1)} %copy-done.2), custom_call_target="tpu_custom_call" | custom-call | tf_op jit(solution)/shard_map/pallas_call | solution.py:52
  (6 shorter events, 0.0 us)
Async XLA Ops:
  1.8 10.0 %collective-permute-start.5 = (bf16[64,256]{1,0:T(8,128)(2,1)S(1)}, bf16[64,256]{1,0:T(8,128)(2,1)S(1)}, u32[]{:S(2)}, u32[]{:S(2)}) collective-permute-start(bf16[64,256]{1,0:T(8,128)(2,1)S(1)} %get-tuple-element.40), channel_id=1, source_target_pairs={{3,0},{2,1},{1,2},{0,3},{7,4},{6,5},{5,6},{4,7},{11,8},{10,9},{9,1... | collective-permute-start | bytes 98312 | tf_op jit(solution)/shard_map/ppermute | solution.py:376
  6.9 4.8 %collective-permute-start.4 = (bf16[64,256]{1,0:T(8,128)(2,1)S(1)}, bf16[64,256]{1,0:T(8,128)(2,1)S(1)}, u32[]{:S(2)}, u32[]{:S(2)}) collective-permute-start(bf16[64,256]{1,0:T(8,128)(2,1)S(1)} %get-tuple-element.40), channel_id=1, source_target_pairs={{2,0},{3,1},{0,2},{1,3},{6,4},{7,5},{4,6},{5,7},{10,8},{11,9},{8,1... | collective-permute-start | bytes 98312 | tf_op jit(solution)/shard_map/ppermute | solution.py:376
  6.9 4.3 %collective-permute-start.3 = (bf16[64,256]{1,0:T(8,128)(2,1)S(1)}, bf16[64,256]{1,0:T(8,128)(2,1)S(1)}, u32[]{:S(2)}, u32[]{:S(2)}) collective-permute-start(bf16[64,256]{1,0:T(8,128)(2,1)S(1)} %get-tuple-element.40), channel_id=1, source_target_pairs={{1,0},{0,1},{3,2},{2,3},{5,4},{4,5},{7,6},{6,7},{9,8},{8,9},{11,10... | collective-permute-start | bytes 98312 | tf_op jit(solution)/shard_map/ppermute | solution.py:376
  7.6 12.7 %collective-permute-start.2 = (bf16[1152,128]{1,0:T(8,128)(2,1)S(1)}, bf16[1152,128]{1,0:T(8,128)(2,1)S(1)}, u32[]{:S(2)}, u32[]{:S(2)}) collective-permute-start(bf16[1152,128]{1,0:T(8,128)(2,1)S(1)} %get-tuple-element.31.refs_0_), channel_id=1, source_target_pairs={{0,4},{4,0},{8,12},{12,8},{1,5},{5,1},{9,13},{13,9},{2,6},{6,2},{1... | collective-permute-start | bytes 884744 | tf_op jit(solution)/shard_map/ppermute | solution.py:358
  7.6 9.9 %collective-permute-start = (bf16[1152,128]{1,0:T(8,128)(2,1)S(1)}, bf16[1152,128]{1,0:T(8,128)(2,1)S(1)}, u32[]{:S(2)}, u32[]{:S(2)}) collective-permute-start(bf16[1152,128]{1,0:T(8,128)(2,1)S(1)} %get-tuple-element.31.refs_0_), channel_id=1, source_target_pairs={{0,8},{4,12},{8,0},{12,4},{1,9},{5,13},{9,1},{13,5},{2,10},{6,14},... | collective-permute-start | bytes 884744 | tf_op jit(solution)/shard_map/ppermute | solution.py:358
  11.8 7.3 %collective-permute-start.6 = (bf16[192,256]{1,0:T(8,128)(2,1)S(1)}, bf16[192,256]{1,0:T(8,128)(2,1)S(1)}, u32[]{:S(2)}, u32[]{:S(2)}) collective-permute-start(bf16[192,256]{1,0:T(8,128)(2,1)S(1)} %constant_dynamic-update-slice_fusion.refs_4_), channel_id=1, source_target_pairs={{0,8},{4,12},{8,0},{12,4},{1,9},{5,13},{9,1},{13,5},{2,10},{6,14},... | collective-permute-start | bytes 294920 | tf_op jit(solution)/shard_map/ppermute | solution.py:358
  17.5 5.1 %collective-permute-start.1 = (bf16[1152,128]{1,0:T(8,128)(2,1)S(1)}, bf16[1152,128]{1,0:T(8,128)(2,1)S(1)}, u32[]{:S(2)}, u32[]{:S(2)}) collective-permute-start(bf16[1152,128]{1,0:T(8,128)(2,1)S(1)} %collective-permute-done.refs_0_.refs_2_), channel_id=1, source_target_pairs={{0,4},{4,0},{8,12},{12,8},{1,5},{5,1},{9,13},{13,9},{2,6},{6,2},{1... | collective-permute-start | bytes 884744 | tf_op jit(solution)/shard_map/ppermute | solution.py:358
  17.5 5.5 %collective-permute-start.7 = (bf16[192,256]{1,0:T(8,128)(2,1)S(1)}, bf16[192,256]{1,0:T(8,128)(2,1)S(1)}, u32[]{:S(2)}, u32[]{:S(2)}) collective-permute-start(bf16[192,256]{1,0:T(8,128)(2,1)S(1)} %constant_dynamic-update-slice_fusion.refs_4_), channel_id=1, source_target_pairs={{0,4},{4,0},{8,12},{12,8},{1,5},{5,1},{9,13},{13,9},{2,6},{6,2},{1... | collective-permute-start | bytes 294920 | tf_op jit(solution)/shard_map/ppermute | solution.py:358
  19.1 3.9 %collective-permute-start.8 = (bf16[192,256]{1,0:T(8,128)(2,1)S(1)}, bf16[192,256]{1,0:T(8,128)(2,1)S(1)}, u32[]{:S(2)}, u32[]{:S(2)}) collective-permute-start(bf16[192,256]{1,0:T(8,128)(2,1)S(1)} %collective-permute-done.6.refs_5_), channel_id=1, source_target_pairs={{0,4},{4,0},{8,12},{12,8},{1,5},{5,1},{9,13},{13,9},{2,6},{6,2},{1... | collective-permute-start | bytes 294920 | tf_op jit(solution)/shard_map/ppermute | solution.py:358
  26.0 2.1 %collective-permute-start.9 = (f32[520,256]{1,0:T(8,128)S(1)}, f32[520,256]{1,0:T(8,128)S(1)}, u32[]{:S(2)}, u32[]{:S(2)}) collective-permute-start(f32[520,256]{1,0:T(8,128)S(1)} %get-tuple-element.48.away_ref), channel_id=1, source_target_pairs={{0,4},{4,0},{8,12},{12,8},{1,5},{5,1},{9,13},{13,9},{2,6},{6,2},{1... | collective-permute-start | bytes 1597448 | tf_op jit(solution)/shard_map/ppermute | solution.py:358
  26.6 18.4 %copy-start = (f32[64,256]{1,0:T(8,128)S(1)}, f32[64,256]{1,0:T(8,128)}, u32[]{:S(2)}) copy-start(f32[64,256]{1,0:T(8,128)} %params_ref.1) | copy-start | bytes 196612
  26.6 18.4 %copy-start.1 = (f32[64,256]{1,0:T(8,128)S(1)}, f32[64,256]{1,0:T(8,128)}, u32[]{:S(2)}) copy-start(f32[64,256]{1,0:T(8,128)} %first_ref.1) | copy-start | bytes 196612
  26.6 18.4 %copy-start.2 = (f32[64,256]{1,0:T(8,128)S(1)}, f32[64,256]{1,0:T(8,128)}, u32[]{:S(2)}) copy-start(f32[64,256]{1,0:T(8,128)} %second_ref.1) | copy-start | bytes 196612
